TPU v7x, 256 devices: a whole 4x4x8 slice. The times are simulated.
256 devices in a mesh: gx: 8 (over x, core), gy: 4 (over y), gz: 8 (over z).
Axes of the slice: x: 4, y: 4, z: 8, core: 2. Of those that a mesh axis runs over, the one named last changes fastest.
Arguments:
- ref_pos: float32 [8, 4, 8, 3, 20480], P('gx', 'gy', 'gz'), may hold values from -6 to 6
- step: float32 [8, 4, 8, 3, 20480], P('gx', 'gy', 'gz'), may hold values from -6 to 6
- inv_mass: float32 [8, 4, 8, 20480], P('gx', 'gy', 'gz'), may hold values from 0.08 to 1
- boundary: int32 [8, 4, 8, 1], P('gx', 'gy', 'gz'), may hold values from 0 to 18432, as said below
- bonds: int32 [8, 4, 8, 2, 24416], P('gx', 'gy', 'gz'), may hold values from 0 to 75775, as said below
Outputs:
- positions: float32 [8, 4, 8, 3, 20480], P('gx', 'gy', 'gz')
- max_deviation: float32 [3], replicated
Inputs may be any that keep to these rules, and one draw needn't show every extreme that they name: Each domain's boundary atoms are the 2048 consecutive atoms from boundary on; boundary is a multiple of 2048. In each domain bond c * 127 + m, for the first 20320 bonds, joins atom 128 * c + m to atom 128 * c + m + 1 (chains of 128 consecutive atoms). Cross bond k (bond 20320 + k) joins the domain's boundary atom boundary + (k mod 2048) (first row) to entry k mod 2048 of one of the 26 neighbour blocks of the extended list (second row), never the centre block; which blocks are reached, and how many bonds each one receives, varies from domain to domain. Every such bond is also listed by that neighbour domain with its two ends swapped, the domain's atom then standing in the neighbour's opposite block.
All inputs are finite; a program needn't handle non-finite values.
Results may differ from a plain program's by a relative error of at most 0.00018.
Values sent between devices are 32-bit elements; how exact they have to be, the bound alone decides.
No kernel may reach another device: no remote copies, remote signals or barrier semaphores. Data moves between devices by JAX's collectives and lax.ppermute only.
A program may use at most 64 MiB of HBM per device.

v0:
```python
import jax
import jax.numpy as jnp
from jax import lax
from jax.sharding import Mesh
from jax.sharding import PartitionSpec as P

ATOMS_DEV = 20480
BOUND = 2048
CROSS_BONDS = 4096
ITERS = 3
LOCAL_BONDS = 20320
GX_GY_GZ = ("gx_0", "gx_1", "gy", "gz")
GX = ("gx_0", "gx_1")


relax_factor = 0.7


def with_halo(cells, sides, width):
    for axis, dim in sides:
        count = lax.axis_size(axis)
        head = lax.slice_in_dim(cells, 0, width, axis=dim)
        tail = lax.slice_in_dim(cells, cells.shape[dim] - width, cells.shape[dim], axis=dim)
        cells = jnp.concatenate(
            [
                lax.ppermute(tail, axis, [(i, (i + 1) % count) for i in range(count)]),
                cells,
                lax.ppermute(head, axis, [((i + 1) % count, i) for i in range(count)]),
            ],
            axis=dim,
        )
    return cells


def one_axis_at_a_time(value, axes):
    for axis in axes:
        value = lax.pmax(value, axis)
    return value


def bond_terms(anchor_left, anchor_right, moved_left, moved_right, inverse_left, inverse_right):
    bond_rest = anchor_left - anchor_right
    bond_now = moved_left - moved_right
    rest_sq = jnp.sum(bond_rest * bond_rest, axis=0)
    now_sq = jnp.sum(bond_now * bond_now, axis=0)
    inner = jnp.sum(bond_rest * bond_now, axis=0)
    excess = now_sq - rest_sq
    deviation = jnp.max(jnp.abs(excess) / (2.0 * jnp.maximum(rest_sq, 1.0)))
    factor = (
        relax_factor * excess / (2.0 * (inverse_left + inverse_right) * jnp.maximum(inner, 1.0))
    )
    return (factor * bond_rest, deviation)


def local(ref_pos, step, inv_mass, boundary, bonds):
    anchor = ref_pos[0, 0, 0]
    current = anchor + step[0, 0, 0]
    inverse = inv_mass[0, 0, 0]
    start = boundary[0, 0, 0, 0]
    chain_count = ATOMS_DEV // 128
    groups = CROSS_BONDS // BOUND
    block_ids = ((bonds[0, 0, 0, 1, LOCAL_BONDS:] - ATOMS_DEV) // BOUND).reshape(groups, BOUND)
    inverse_chain = inverse.reshape(chain_count, 128)
    anchor_chain = anchor.reshape(3, chain_count, 128)
    inverse_slot = lax.dynamic_slice_in_dim(inverse, start, BOUND, 0)
    anchor_slot = lax.dynamic_slice_in_dim(anchor, start, BOUND, 1)

    def rims(values_in):
        return lax.dynamic_slice_in_dim(values_in, start, BOUND, 1)[:, None, None, None, :]

    def spread(blocks):
        return blocks.reshape(blocks.shape[0], 27, BOUND)

    def select(far_rows):
        picked = jnp.zeros((far_rows.shape[0], groups, BOUND), jnp.float32)
        for block in range(27):
            if block == 13:
                continue
            picked = jnp.where((block_ids == block)[None], far_rows[:, block][:, None, :], picked)
        return picked

    fixed = spread(
        with_halo(
            rims(jnp.concatenate([anchor, inverse[None]], axis=0)),
            ((GX, 1), ("gy", 2), ("gz", 3)),
            1,
        )
    )
    far_anchor = fixed[:3]
    far_inverse = fixed[3]
    reports = []
    for iteration in range(ITERS):
        far_moved = spread(with_halo(rims(current), ((GX, 1), ("gy", 2), ("gz", 3)), 1))
        moved_chain = current.reshape(3, chain_count, 128)
        local_term, local_dev = bond_terms(
            anchor_chain[:, :, :-1],
            anchor_chain[:, :, 1:],
            moved_chain[:, :, :-1],
            moved_chain[:, :, 1:],
            inverse_chain[:, :-1],
            inverse_chain[:, 1:],
        )
        zeros_col = jnp.zeros((3, chain_count, 1), jnp.float32)
        delta = jnp.concatenate([-local_term * inverse_chain[:, :-1], zeros_col], axis=2)
        delta = delta + jnp.concatenate([zeros_col, local_term * inverse_chain[:, 1:]], axis=2)
        local_delta, local_dev = (delta.reshape(3, ATOMS_DEV), local_dev)
        moved_slot = lax.dynamic_slice_in_dim(current, start, BOUND, 1)
        term, cross_dev = bond_terms(
            anchor_slot[:, None, :],
            select(far_anchor),
            moved_slot[:, None, :],
            select(far_moved),
            inverse_slot[None, :],
            select(far_inverse[None])[0],
        )
        cross_delta, cross_dev = (-jnp.sum(term, axis=1) * inverse_slot, cross_dev)
        deviation = jnp.maximum(local_dev, cross_dev)
        updated = current + local_delta
        edge_now = lax.dynamic_slice_in_dim(updated, start, BOUND, 1) + cross_delta
        current = lax.dynamic_update_slice_in_dim(updated, edge_now, start, 1)
        reports.append(one_axis_at_a_time(deviation, GX_GY_GZ))
    summary = jnp.stack(reports)
    return (current[None, None, None], summary)


def solution(mesh):
    finer = Mesh(
        mesh.devices.reshape(4, 2, mesh.shape["gy"], mesh.shape["gz"]), ("gx_0", "gx_1", "gy", "gz")
    )
    placed = (
        P(GX, "gy", "gz", None, None),
        P(GX, "gy", "gz", None, None),
        P(GX, "gy", "gz", None),
        P(GX, "gy", "gz", None),
        P(GX, "gy", "gz", None, None),
    )
    return jax.shard_map(
        local,
        mesh=finer,
        in_specs=placed,
        out_specs=(P(GX, "gy", "gz", None, None), P()),
        check_vma=False,
    )
```

profile of v0, /device:TPU:8, one launch (start us, length us, event | category | flops | bytes accessed | tf_op | source)
XLA Modules:
  0.0 135.4 jit_solution(5466381230885481899)
XLA Ops:
  1.3 1.2 copy.29
  2.6 2.2 %collective-permute-start.7 = (f32[4,1,1,1,2048]{4,0,3,2,1:T(4,128)S(1)}, f32[4,1,1,1,2048]{4,0,3,2,1:T(4,128)S(1)}, u32[]{:S(2)}, u32[]{:S(2)}) collective-permute-start(f32[4,1,1,1,2048]{4,0,3,2,1:T(4,128)S(1)} %fusion.4), channel_id=1, source_target_pairs={{32,0},{64,32},{96,64},{128,96},{160,128},{192,160},{224,192},{0,2... | collective-permute-start | bytes 98312 | tf_op jit(solution)/shard_map/ppermute | solution.py:28
  5.9 3.0 %collective-permute-start.1 = (f32[3,1,1,1,2048]{4,0,3,2,1:T(4,128)S(1)}, f32[3,1,1,1,2048]{4,0,3,2,1:T(4,128)S(1)}, u32[]{:S(2)}, u32[]{:S(2)}) collective-permute-start(f32[3,1,1,1,2048]{4,0,3,2,1:T(4,128)S(1)} %fusion.13), channel_id=1, source_target_pairs={{32,0},{64,32},{96,64},{128,96},{160,128},{192,160},{224,192},{0,2... | collective-permute-start | bytes 73736 | tf_op jit(solution)/shard_map/ppermute | solution.py:28
  9.1 0.9 add_reduce_fusion
  10.5 3.0 %collective-permute-done = f32[3,1,1,1,2048]{4,0,3,2,1:T(4,128)S(1)} collective-permute-done((f32[3,1,1,1,2048]{4,0,3,2,1:T(4,128)S(1)}, f32[3,1,1,1,2048]{4,0,3,2,1:T(4,128)S(1)}, u32[]{:S(2)}, u32[]{:S(2)}) %collective-permute-start) | collective-permute-done | bytes 24608 | tf_op jit(solution)/shard_map/ppermute | solution.py:26
  13.5 0.5 collective-permute-start.3
  14.0 1.6 %collective-permute-start.2 = (f32[3,3,1,1,2048]{4,0,3,2,1:T(4,128)S(1)}, f32[3,3,1,1,2048]{4,0,3,2,1:T(4,128)S(1)}, u32[]{:S(2)}, u32[]{:S(2)}) collective-permute-start(f32[3,3,1,1,2048]{4,0,3,2,1:T(4,128)S(1)} %pad_maximum_fusion.9), channel_id=1, source_target_pairs={{0,8},{8,16},{16,24},{24,0},{1,9},{9,17},{17,25},{25,1},{2,10},{10... | collective-permute-start | bytes 221192 | tf_op jit(solution)/shard_map/ppermute | solution.py:26
  15.6 1.5 %collective-permute-start.9 = (f32[4,3,1,1,2048]{4,0,3,2,1:T(4,128)S(1)}, f32[4,3,1,1,2048]{4,0,3,2,1:T(4,128)S(1)}, u32[]{:S(2)}, u32[]{:S(2)}) collective-permute-start(f32[4,3,1,1,2048]{4,0,3,2,1:T(4,128)S(1)} %pad_maximum_fusion.10), channel_id=1, source_target_pairs={{8,0},{16,8},{24,16},{0,24},{9,1},{17,9},{25,17},{1,25},{10,2},{18... | collective-permute-start | bytes 294920 | tf_op jit(solution)/shard_map/ppermute | solution.py:28
  17.1 0.6 collective-permute-start.8
  18.2 1.4 %collective-permute-done.2 = f32[3,3,1,1,2048]{4,0,3,2,1:T(4,128)S(1)} collective-permute-done((f32[3,3,1,1,2048]{4,0,3,2,1:T(4,128)S(1)}, f32[3,3,1,1,2048]{4,0,3,2,1:T(4,128)S(1)}, u32[]{:S(2)}, u32[]{:S(2)}) %collective-permute-start.2) | collective-permute-done | bytes 73760 | tf_op jit(solution)/shard_map/ppermute | solution.py:26
  19.7 5.9 %collective-permute-start.5 = (f32[3,3,3,1,2048]{4,0,3,2,1:T(4,128)S(1)}, f32[3,3,3,1,2048]{4,0,3,2,1:T(4,128)S(1)}, u32[]{:S(2)}, u32[]{:S(2)}) collective-permute-start(f32[3,3,3,1,2048]{4,0,3,2,1:T(4,128)S(1)} %pad_maximum_fusion.4), channel_id=1, source_target_pairs={{1,0},{2,1},{3,2},{4,3},{5,4},{6,5},{7,6},{0,7},{9,8},{10,9},{11,1... | collective-permute-start | bytes 663560 | tf_op jit(solution)/shard_map/ppermute | solution.py:28
  25.7 3.3 %collective-permute-start.11 = (f32[4,3,3,1,2048]{4,0,3,2,1:T(4,128)S(1)}, f32[4,3,3,1,2048]{4,0,3,2,1:T(4,128)S(1)}, u32[]{:S(2)}, u32[]{:S(2)}) collective-permute-start(f32[4,3,3,1,2048]{4,0,3,2,1:T(4,128)S(1)} %pad_maximum_fusion.5), channel_id=1, source_target_pairs={{1,0},{2,1},{3,2},{4,3},{5,4},{6,5},{7,6},{0,7},{9,8},{10,9},{11,1... | collective-permute-start | bytes 884744 | tf_op jit(solution)/shard_map/ppermute | solution.py:28
  29.0 1.7 %collective-permute-done.5 = f32[3,3,3,1,2048]{4,0,3,2,1:T(4,128)S(1)} collective-permute-done((f32[3,3,3,1,2048]{4,0,3,2,1:T(4,128)S(1)}, f32[3,3,3,1,2048]{4,0,3,2,1:T(4,128)S(1)}, u32[]{:S(2)}, u32[]{:S(2)}) %collective-permute-start.5) | collective-permute-done | bytes 221216 | tf_op jit(solution)/shard_map/ppermute | solution.py:28
  30.7 3.4 %collective-permute-done.4 = f32[3,3,3,1,2048]{4,0,3,2,1:T(4,128)S(1)} collective-permute-done((f32[3,3,3,1,2048]{4,0,3,2,1:T(4,128)S(1)}, f32[3,3,3,1,2048]{4,0,3,2,1:T(4,128)S(1)}, u32[]{:S(2)}, u32[]{:S(2)}) %collective-permute-start.4) | collective-permute-done | bytes 221216 | tf_op jit(solution)/shard_map/ppermute | solution.py:26
  34.6 2.7 %collective-permute-done.10 = f32[4,3,3,1,2048]{4,0,3,2,1:T(4,128)S(1)} collective-permute-done((f32[4,3,3,1,2048]{4,0,3,2,1:T(4,128)S(1)}, f32[4,3,3,1,2048]{4,0,3,2,1:T(4,128)S(1)}, u32[]{:S(2)}, u32[]{:S(2)}) %collective-permute-start.10) | collective-permute-done | bytes 294944 | tf_op jit(solution)/shard_map/ppermute | solution.py:26
  38.1 1.3 multiply_reduce_fusion.15
  40.0 0.5 dynamic_update_slice.10
  40.5 3.6 %collective-permute-start.13 = (f32[3,1,1,1,2048]{4,0,3,2,1:T(4,128)S(1)}, f32[3,1,1,1,2048]{4,0,3,2,1:T(4,128)S(1)}, u32[]{:S(2)}, u32[]{:S(2)}) collective-permute-start(f32[3,1,1,1,2048]{4,0,3,2,1:T(4,128)S(1)} %fusion.12), channel_id=1, source_target_pairs={{32,0},{64,32},{96,64},{128,96},{160,128},{192,160},{224,192},{0,2... | collective-permute-start | bytes 73736 | tf_op jit(solution)/shard_map/ppermute | solution.py:28
  44.6 1.1 collective-permute-done.13
  45.7 3.0 %collective-permute-done.12 = f32[3,1,1,1,2048]{4,0,3,2,1:T(4,128)S(1)} collective-permute-done((f32[3,1,1,1,2048]{4,0,3,2,1:T(4,128)S(1)}, f32[3,1,1,1,2048]{4,0,3,2,1:T(4,128)S(1)}, u32[]{:S(2)}, u32[]{:S(2)}) %collective-permute-start.12) | collective-permute-done | bytes 24608 | tf_op jit(solution)/shard_map/ppermute | solution.py:26
  48.7 2.7 %collective-permute-start.15 = (f32[3,3,1,1,2048]{4,0,3,2,1:T(4,128)S(1)}, f32[3,3,1,1,2048]{4,0,3,2,1:T(4,128)S(1)}, u32[]{:S(2)}, u32[]{:S(2)}) collective-permute-start(f32[3,3,1,1,2048]{4,0,3,2,1:T(4,128)S(1)} %pad_maximum_fusion.11), channel_id=1, source_target_pairs={{8,0},{16,8},{24,16},{0,24},{9,1},{17,9},{25,17},{1,25},{10,2},{18... | collective-permute-start | bytes 221192 | tf_op jit(solution)/shard_map/ppermute | solution.py:28
  51.7 2.0 %collective-permute-done.15 = f32[3,3,1,1,2048]{4,0,3,2,1:T(4,128)S(1)} collective-permute-done((f32[3,3,1,1,2048]{4,0,3,2,1:T(4,128)S(1)}, f32[3,3,1,1,2048]{4,0,3,2,1:T(4,128)S(1)}, u32[]{:S(2)}, u32[]{:S(2)}) %collective-permute-start.15) | collective-permute-done | bytes 73760 | tf_op jit(solution)/shard_map/ppermute | solution.py:28
  53.7 2.4 %collective-permute-done.14 = f32[3,3,1,1,2048]{4,0,3,2,1:T(4,128)S(1)} collective-permute-done((f32[3,3,1,1,2048]{4,0,3,2,1:T(4,128)S(1)}, f32[3,3,1,1,2048]{4,0,3,2,1:T(4,128)S(1)}, u32[]{:S(2)}, u32[]{:S(2)}) %collective-permute-start.14) | collective-permute-done | bytes 73760 | tf_op jit(solution)/shard_map/ppermute | solution.py:26
  56.1 0.6 collective-permute-start.17
  56.7 1.5 %collective-permute-start.16 = (f32[3,3,3,1,2048]{4,0,3,2,1:T(4,128)S(1)}, f32[3,3,3,1,2048]{4,0,3,2,1:T(4,128)S(1)}, u32[]{:S(2)}, u32[]{:S(2)}) collective-permute-start(f32[3,3,3,1,2048]{4,0,3,2,1:T(4,128)S(1)} %pad_maximum_fusion.6), channel_id=1, source_target_pairs={{0,1},{1,2},{2,3},{3,4},{4,5},{5,6},{6,7},{7,0},{8,9},{9,10},{10,1... | collective-permute-start | bytes 663560 | tf_op jit(solution)/shard_map/ppermute | solution.py:26
  58.3 4.6 %collective-permute-done.17 = f32[3,3,3,1,2048]{4,0,3,2,1:T(4,128)S(1)} collective-permute-done((f32[3,3,3,1,2048]{4,0,3,2,1:T(4,128)S(1)}, f32[3,3,3,1,2048]{4,0,3,2,1:T(4,128)S(1)}, u32[]{:S(2)}, u32[]{:S(2)}) %collective-permute-start.17) | collective-permute-done | bytes 221216 | tf_op jit(solution)/shard_map/ppermute | solution.py:28
  62.9 1.7 %collective-permute-done.16 = f32[3,3,3,1,2048]{4,0,3,2,1:T(4,128)S(1)} collective-permute-done((f32[3,3,3,1,2048]{4,0,3,2,1:T(4,128)S(1)}, f32[3,3,3,1,2048]{4,0,3,2,1:T(4,128)S(1)}, u32[]{:S(2)}, u32[]{:S(2)}) %collective-permute-start.16) | collective-permute-done | bytes 221216 | tf_op jit(solution)/shard_map/ppermute | solution.py:26
  65.2 0.5 multiply_reduce_fusion.12
  65.9 0.5 dynamic_update_slice.11
  66.5 0.5 collective-permute-start.18
  67.2 0.7 fusion
  68.1 3.0 %collective-permute-done.18 = f32[3,1,1,1,2048]{4,0,3,2,1:T(4,128)S(1)} collective-permute-done((f32[3,1,1,1,2048]{4,0,3,2,1:T(4,128)S(1)}, f32[3,1,1,1,2048]{4,0,3,2,1:T(4,128)S(1)}, u32[]{:S(2)}, u32[]{:S(2)}) %collective-permute-start.18) | collective-permute-done | bytes 24608 | tf_op jit(solution)/shard_map/ppermute | solution.py:26
  71.1 3.1 %collective-permute-start.21 = (f32[3,3,1,1,2048]{4,0,3,2,1:T(4,128)S(1)}, f32[3,3,1,1,2048]{4,0,3,2,1:T(4,128)S(1)}, u32[]{:S(2)}, u32[]{:S(2)}) collective-permute-start(f32[3,3,1,1,2048]{4,0,3,2,1:T(4,128)S(1)} %pad_maximum_fusion.12), channel_id=1, source_target_pairs={{8,0},{16,8},{24,16},{0,24},{9,1},{17,9},{25,17},{1,25},{10,2},{18... | collective-permute-start | bytes 221192 | tf_op jit(solution)/shard_map/ppermute | solution.py:28
  74.4 2.0 %collective-permute-done.21 = f32[3,3,1,1,2048]{4,0,3,2,1:T(4,128)S(1)} collective-permute-done((f32[3,3,1,1,2048]{4,0,3,2,1:T(4,128)S(1)}, f32[3,3,1,1,2048]{4,0,3,2,1:T(4,128)S(1)}, u32[]{:S(2)}, u32[]{:S(2)}) %collective-permute-start.21) | collective-permute-done | bytes 73760 | tf_op jit(solution)/shard_map/ppermute | solution.py:28
  76.4 2.4 %collective-permute-done.20 = f32[3,3,1,1,2048]{4,0,3,2,1:T(4,128)S(1)} collective-permute-done((f32[3,3,1,1,2048]{4,0,3,2,1:T(4,128)S(1)}, f32[3,3,1,1,2048]{4,0,3,2,1:T(4,128)S(1)}, u32[]{:S(2)}, u32[]{:S(2)}) %collective-permute-start.20) | collective-permute-done | bytes 73760 | tf_op jit(solution)/shard_map/ppermute | solution.py:26
  78.9 0.6 collective-permute-start.23
  79.5 1.5 %collective-permute-start.22 = (f32[3,3,3,1,2048]{4,0,3,2,1:T(4,128)S(1)}, f32[3,3,3,1,2048]{4,0,3,2,1:T(4,128)S(1)}, u32[]{:S(2)}, u32[]{:S(2)}) collective-permute-start(f32[3,3,3,1,2048]{4,0,3,2,1:T(4,128)S(1)} %pad_maximum_fusion.7), channel_id=1, source_target_pairs={{0,1},{1,2},{2,3},{3,4},{4,5},{5,6},{6,7},{7,0},{8,9},{9,10},{10,1... | collective-permute-start | bytes 663560 | tf_op jit(solution)/shard_map/ppermute | solution.py:26
  81.1 4.6 %collective-permute-done.23 = f32[3,3,3,1,2048]{4,0,3,2,1:T(4,128)S(1)} collective-permute-done((f32[3,3,3,1,2048]{4,0,3,2,1:T(4,128)S(1)}, f32[3,3,3,1,2048]{4,0,3,2,1:T(4,128)S(1)}, u32[]{:S(2)}, u32[]{:S(2)}) %collective-permute-start.23) | collective-permute-done | bytes 221216 | tf_op jit(solution)/shard_map/ppermute | solution.py:28
  85.7 1.7 %collective-permute-done.22 = f32[3,3,3,1,2048]{4,0,3,2,1:T(4,128)S(1)} collective-permute-done((f32[3,3,3,1,2048]{4,0,3,2,1:T(4,128)S(1)}, f32[3,3,3,1,2048]{4,0,3,2,1:T(4,128)S(1)}, u32[]{:S(2)}, u32[]{:S(2)}) %collective-permute-start.22) | collective-permute-done | bytes 221216 | tf_op jit(solution)/shard_map/ppermute | solution.py:26
  87.9 0.5 multiply_reduce_fusion.9
  88.5 0.7 fusion.5
  93.2 0.5 dynamic_update_slice.12
  93.7 0.9 copy.8
  94.6 9.6 %all-reduce.8 = (f32[]{:T(128)}, f32[]{:T(128)}, f32[]{:T(128)}) all-reduce(f32[]{:T(128)S(6)} %max.83, f32[]{:T(128)S(6)} %max.82, f32[]{:T(128)S(6)} %max.81), channel_id=1, replica_groups=mesh['gx_0'=4,'gx_1'=2,'gy'=4,'gz'=8] {'gx_0'}, use_global_device_ids=true, to_apply=%region_31.32 | all-reduce | flops 3 | bytes 24 | tf_op jit(solution)/shard_map/pmax | solution.py:37
  104.2 3.1 %all-reduce.9 = (f32[]{:T(128)}, f32[]{:T(128)}, f32[]{:T(128)}) all-reduce(f32[]{:T(128)} %get-tuple-element.30, f32[]{:T(128)} %get-tuple-element.31, f32[]{:T(128)} %get-tuple-element.32), channel_id=1, replica_groups=mesh['gx_0'=4,'gx_1'=2,'gy'=4,'gz'=8] {'gx_1'}, use_global_device_ids=true, to_apply=%region_32.33 | all-reduce | flops 3 | bytes 24 | tf_op jit(solution)/shard_map/pmax | solution.py:37
  107.4 10.4 %all-reduce.7 = (f32[]{:T(128)}, f32[]{:T(128)}, f32[]{:T(128)}) all-reduce(f32[]{:T(128)} %get-tuple-element.33, f32[]{:T(128)} %get-tuple-element.34, f32[]{:T(128)} %get-tuple-element.35), channel_id=1, replica_groups=mesh['gx_0'=4,'gx_1'=2,'gy'=4,'gz'=8] {'gy'}, use_global_device_ids=true, to_apply=%region_33.34 | all-reduce | flops 3 | bytes 24 | tf_op jit(solution)/shard_map/pmax | solution.py:37
  117.8 15.1 %all-reduce.6 = (f32[1]{0:T(128)}, f32[1]{0:T(128)}, f32[1]{0:T(128)}) all-reduce(f32[1]{0:T(128)} %bitcast.149, f32[1]{0:T(128)} %bitcast.148, f32[1]{0:T(128)} %bitcast.147), channel_id=1, replica_groups=mesh['gx_0'=4,'gx_1'=2,'gy'=4,'gz'=8] {'gz'}, use_global_device_ids=true, to_apply=%region_34.35 | all-reduce | flops 3 | bytes 24 | tf_op jit(solution)/shard_map/pmax | solution.py:37
  132.9 2.5 %pad_maximum_fusion.13 = f32[3]{0:T(128)} fusion(f32[1]{0:T(128)} %get-tuple-element.24, f32[1]{0:T(128)} %get-tuple-element.25, f32[1]{0:T(128)} %get-tuple-element.26), kind=kLoop, calls=%fused_computation.224 | loop fusion | flops 6 | bytes 24 | tf_op jit(solution)/shard_map/stack | solution.py:122
  (82 shorter events, 7.4 us)
Async XLA Ops:
  1.3 1.2 copy-start.1
  1.3 3.5 %copy-start.2 = (f32[1,1,1,3,20480]{4,2,3,1,0:T(1,128)S(1)}, f32[1,1,1,3,20480]{4,2,3,1,0:T(1,128)}, u32[]{:S(2)}) copy-start(f32[1,1,1,3,20480]{4,2,3,1,0:T(1,128)} %param.6) | copy-start | bytes 737284
  2.5 2.4 %copy-start = (f32[1,1,1,3,20480]{4,2,3,1,0:T(1,128)S(1)}, f32[1,1,1,3,20480]{4,2,3,1,0:T(1,128)}, u32[]{:S(2)}) copy-start(f32[1,1,1,3,20480]{4,2,3,1,0:T(1,128)} %param.5) | copy-start | bytes 737284
  2.6 13.0 %collective-permute-start.7 = (f32[4,1,1,1,2048]{4,0,3,2,1:T(4,128)S(1)}, f32[4,1,1,1,2048]{4,0,3,2,1:T(4,128)S(1)}, u32[]{:S(2)}, u32[]{:S(2)}) collective-permute-start(f32[4,1,1,1,2048]{4,0,3,2,1:T(4,128)S(1)} %fusion.4), channel_id=1, source_target_pairs={{32,0},{64,32},{96,64},{128,96},{160,128},{192,160},{224,192},{0,2... | collective-permute-start | bytes 98312 | tf_op jit(solution)/shard_map/ppermute | solution.py:28
  4.8 10.8 %collective-permute-start.6 = (f32[4,1,1,1,2048]{4,0,3,2,1:T(4,128)S(1)}, f32[4,1,1,1,2048]{4,0,3,2,1:T(4,128)S(1)}, u32[]{:S(2)}, u32[]{:S(2)}) collective-permute-start(f32[4,1,1,1,2048]{4,0,3,2,1:T(4,128)S(1)} %fusion.4), channel_id=1, source_target_pairs={{0,32},{32,64},{64,96},{96,128},{128,160},{160,192},{192,224},{224... | collective-permute-start | bytes 98312 | tf_op jit(solution)/shard_map/ppermute | solution.py:26
  5.9 4.6 %collective-permute-start.1 = (f32[3,1,1,1,2048]{4,0,3,2,1:T(4,128)S(1)}, f32[3,1,1,1,2048]{4,0,3,2,1:T(4,128)S(1)}, u32[]{:S(2)}, u32[]{:S(2)}) collective-permute-start(f32[3,1,1,1,2048]{4,0,3,2,1:T(4,128)S(1)} %fusion.13), channel_id=1, source_target_pairs={{32,0},{64,32},{96,64},{128,96},{160,128},{192,160},{224,192},{0,2... | collective-permute-start | bytes 73736 | tf_op jit(solution)/shard_map/ppermute | solution.py:28
  8.9 4.6 %collective-permute-start = (f32[3,1,1,1,2048]{4,0,3,2,1:T(4,128)S(1)}, f32[3,1,1,1,2048]{4,0,3,2,1:T(4,128)S(1)}, u32[]{:S(2)}, u32[]{:S(2)}) collective-permute-start(f32[3,1,1,1,2048]{4,0,3,2,1:T(4,128)S(1)} %fusion.13), channel_id=1, source_target_pairs={{0,32},{32,64},{64,96},{96,128},{128,160},{160,192},{192,224},{224... | collective-permute-start | bytes 73736 | tf_op jit(solution)/shard_map/ppermute | solution.py:26
  13.5 4.7 %collective-permute-start.3 = (f32[3,3,1,1,2048]{4,0,3,2,1:T(4,128)S(1)}, f32[3,3,1,1,2048]{4,0,3,2,1:T(4,128)S(1)}, u32[]{:S(2)}, u32[]{:S(2)}) collective-permute-start(f32[3,3,1,1,2048]{4,0,3,2,1:T(4,128)S(1)} %pad_maximum_fusion.9), channel_id=1, source_target_pairs={{8,0},{16,8},{24,16},{0,24},{9,1},{17,9},{25,17},{1,25},{10,2},{18... | collective-permute-start | bytes 221192 | tf_op jit(solution)/shard_map/ppermute | solution.py:28
  14.0 5.6 %collective-permute-start.2 = (f32[3,3,1,1,2048]{4,0,3,2,1:T(4,128)S(1)}, f32[3,3,1,1,2048]{4,0,3,2,1:T(4,128)S(1)}, u32[]{:S(2)}, u32[]{:S(2)}) collective-permute-start(f32[3,3,1,1,2048]{4,0,3,2,1:T(4,128)S(1)} %pad_maximum_fusion.9), channel_id=1, source_target_pairs={{0,8},{8,16},{16,24},{24,0},{1,9},{9,17},{17,25},{25,1},{2,10},{10... | collective-permute-start | bytes 221192 | tf_op jit(solution)/shard_map/ppermute | solution.py:26
  15.6 10.0 %collective-permute-start.9 = (f32[4,3,1,1,2048]{4,0,3,2,1:T(4,128)S(1)}, f32[4,3,1,1,2048]{4,0,3,2,1:T(4,128)S(1)}, u32[]{:S(2)}, u32[]{:S(2)}) collective-permute-start(f32[4,3,1,1,2048]{4,0,3,2,1:T(4,128)S(1)} %pad_maximum_fusion.10), channel_id=1, source_target_pairs={{8,0},{16,8},{24,16},{0,24},{9,1},{17,9},{25,17},{1,25},{10,2},{18... | collective-permute-start | bytes 294920 | tf_op jit(solution)/shard_map/ppermute | solution.py:28
  17.1 8.5 %collective-permute-start.8 = (f32[4,3,1,1,2048]{4,0,3,2,1:T(4,128)S(1)}, f32[4,3,1,1,2048]{4,0,3,2,1:T(4,128)S(1)}, u32[]{:S(2)}, u32[]{:S(2)}) collective-permute-start(f32[4,3,1,1,2048]{4,0,3,2,1:T(4,128)S(1)} %pad_maximum_fusion.10), channel_id=1, source_target_pairs={{0,8},{8,16},{16,24},{24,0},{1,9},{9,17},{17,25},{25,1},{2,10},{10... | collective-permute-start | bytes 294920 | tf_op jit(solution)/shard_map/ppermute | solution.py:26
  19.7 11.0 %collective-permute-start.5 = (f32[3,3,3,1,2048]{4,0,3,2,1:T(4,128)S(1)}, f32[3,3,3,1,2048]{4,0,3,2,1:T(4,128)S(1)}, u32[]{:S(2)}, u32[]{:S(2)}) collective-permute-start(f32[3,3,3,1,2048]{4,0,3,2,1:T(4,128)S(1)} %pad_maximum_fusion.4), channel_id=1, source_target_pairs={{1,0},{2,1},{3,2},{4,3},{5,4},{6,5},{7,6},{0,7},{9,8},{10,9},{11,1... | collective-permute-start | bytes 663560 | tf_op jit(solution)/shard_map/ppermute | solution.py:28
  25.6 8.5 %collective-permute-start.4 = (f32[3,3,3,1,2048]{4,0,3,2,1:T(4,128)S(1)}, f32[3,3,3,1,2048]{4,0,3,2,1:T(4,128)S(1)}, u32[]{:S(2)}, u32[]{:S(2)}) collective-permute-start(f32[3,3,3,1,2048]{4,0,3,2,1:T(4,128)S(1)} %pad_maximum_fusion.4), channel_id=1, source_target_pairs={{0,1},{1,2},{2,3},{3,4},{4,5},{5,6},{6,7},{7,0},{8,9},{9,10},{10,1... | collective-permute-start | bytes 663560 | tf_op jit(solution)/shard_map/ppermute | solution.py:26
  25.7 8.9 %collective-permute-start.11 = (f32[4,3,3,1,2048]{4,0,3,2,1:T(4,128)S(1)}, f32[4,3,3,1,2048]{4,0,3,2,1:T(4,128)S(1)}, u32[]{:S(2)}, u32[]{:S(2)}) collective-permute-start(f32[4,3,3,1,2048]{4,0,3,2,1:T(4,128)S(1)} %pad_maximum_fusion.5), channel_id=1, source_target_pairs={{1,0},{2,1},{3,2},{4,3},{5,4},{6,5},{7,6},{0,7},{9,8},{10,9},{11,1... | collective-permute-start | bytes 884744 | tf_op jit(solution)/shard_map/ppermute | solution.py:28
  29.0 8.3 %collective-permute-start.10 = (f32[4,3,3,1,2048]{4,0,3,2,1:T(4,128)S(1)}, f32[4,3,3,1,2048]{4,0,3,2,1:T(4,128)S(1)}, u32[]{:S(2)}, u32[]{:S(2)}) collective-permute-start(f32[4,3,3,1,2048]{4,0,3,2,1:T(4,128)S(1)} %pad_maximum_fusion.5), channel_id=1, source_target_pairs={{0,1},{1,2},{2,3},{3,4},{4,5},{5,6},{6,7},{7,0},{8,9},{9,10},{10,1... | collective-permute-start | bytes 884744 | tf_op jit(solution)/shard_map/ppermute | solution.py:26
  40.5 5.2 %collective-permute-start.13 = (f32[3,1,1,1,2048]{4,0,3,2,1:T(4,128)S(1)}, f32[3,1,1,1,2048]{4,0,3,2,1:T(4,128)S(1)}, u32[]{:S(2)}, u32[]{:S(2)}) collective-permute-start(f32[3,1,1,1,2048]{4,0,3,2,1:T(4,128)S(1)} %fusion.12), channel_id=1, source_target_pairs={{32,0},{64,32},{96,64},{128,96},{160,128},{192,160},{224,192},{0,2... | collective-permute-start | bytes 73736 | tf_op jit(solution)/shard_map/ppermute | solution.py:28
  44.1 4.6 %collective-permute-start.12 = (f32[3,1,1,1,2048]{4,0,3,2,1:T(4,128)S(1)}, f32[3,1,1,1,2048]{4,0,3,2,1:T(4,128)S(1)}, u32[]{:S(2)}, u32[]{:S(2)}) collective-permute-start(f32[3,1,1,1,2048]{4,0,3,2,1:T(4,128)S(1)} %fusion.12), channel_id=1, source_target_pairs={{0,32},{32,64},{64,96},{96,128},{128,160},{160,192},{192,224},{224... | collective-permute-start | bytes 73736 | tf_op jit(solution)/shard_map/ppermute | solution.py:26
  48.7 5.0 %collective-permute-start.15 = (f32[3,3,1,1,2048]{4,0,3,2,1:T(4,128)S(1)}, f32[3,3,1,1,2048]{4,0,3,2,1:T(4,128)S(1)}, u32[]{:S(2)}, u32[]{:S(2)}) collective-permute-start(f32[3,3,1,1,2048]{4,0,3,2,1:T(4,128)S(1)} %pad_maximum_fusion.11), channel_id=1, source_target_pairs={{8,0},{16,8},{24,16},{0,24},{9,1},{17,9},{25,17},{1,25},{10,2},{18... | collective-permute-start | bytes 221192 | tf_op jit(solution)/shard_map/ppermute | solution.py:28
  51.4 4.6 %collective-permute-start.14 = (f32[3,3,1,1,2048]{4,0,3,2,1:T(4,128)S(1)}, f32[3,3,1,1,2048]{4,0,3,2,1:T(4,128)S(1)}, u32[]{:S(2)}, u32[]{:S(2)}) collective-permute-start(f32[3,3,1,1,2048]{4,0,3,2,1:T(4,128)S(1)} %pad_maximum_fusion.11), channel_id=1, source_target_pairs={{0,8},{8,16},{16,24},{24,0},{1,9},{9,17},{17,25},{25,1},{2,10},{10... | collective-permute-start | bytes 221192 | tf_op jit(solution)/shard_map/ppermute | solution.py:26
  56.1 6.8 %collective-permute-start.17 = (f32[3,3,3,1,2048]{4,0,3,2,1:T(4,128)S(1)}, f32[3,3,3,1,2048]{4,0,3,2,1:T(4,128)S(1)}, u32[]{:S(2)}, u32[]{:S(2)}) collective-permute-start(f32[3,3,3,1,2048]{4,0,3,2,1:T(4,128)S(1)} %pad_maximum_fusion.6), channel_id=1, source_target_pairs={{1,0},{2,1},{3,2},{4,3},{5,4},{6,5},{7,6},{0,7},{9,8},{10,9},{11,1... | collective-permute-start | bytes 663560 | tf_op jit(solution)/shard_map/ppermute | solution.py:28
  56.7 7.9 %collective-permute-start.16 = (f32[3,3,3,1,2048]{4,0,3,2,1:T(4,128)S(1)}, f32[3,3,3,1,2048]{4,0,3,2,1:T(4,128)S(1)}, u32[]{:S(2)}, u32[]{:S(2)}) collective-permute-start(f32[3,3,3,1,2048]{4,0,3,2,1:T(4,128)S(1)} %pad_maximum_fusion.6), channel_id=1, source_target_pairs={{0,1},{1,2},{2,3},{3,4},{4,5},{5,6},{6,7},{7,0},{8,9},{9,10},{10,1... | collective-permute-start | bytes 663560 | tf_op jit(solution)/shard_map/ppermute | solution.py:26
  66.5 1.6 %collective-permute-start.19 = (f32[3,1,1,1,2048]{4,0,3,2,1:T(4,128)S(1)}, f32[3,1,1,1,2048]{4,0,3,2,1:T(4,128)S(1)}, u32[]{:S(2)}, u32[]{:S(2)}) collective-permute-start(f32[3,1,1,1,2048]{4,0,3,2,1:T(4,128)S(1)} %fusion.11), channel_id=1, source_target_pairs={{32,0},{64,32},{96,64},{128,96},{160,128},{192,160},{224,192},{0,2... | collective-permute-start | bytes 73736 | tf_op jit(solution)/shard_map/ppermute | solution.py:28
  66.5 4.6 %collective-permute-start.18 = (f32[3,1,1,1,2048]{4,0,3,2,1:T(4,128)S(1)}, f32[3,1,1,1,2048]{4,0,3,2,1:T(4,128)S(1)}, u32[]{:S(2)}, u32[]{:S(2)}) collective-permute-start(f32[3,1,1,1,2048]{4,0,3,2,1:T(4,128)S(1)} %fusion.11), channel_id=1, source_target_pairs={{0,32},{32,64},{64,96},{96,128},{128,160},{160,192},{192,224},{224... | collective-permute-start | bytes 73736 | tf_op jit(solution)/shard_map/ppermute | solution.py:26
  71.1 5.3 %collective-permute-start.21 = (f32[3,3,1,1,2048]{4,0,3,2,1:T(4,128)S(1)}, f32[3,3,1,1,2048]{4,0,3,2,1:T(4,128)S(1)}, u32[]{:S(2)}, u32[]{:S(2)}) collective-permute-start(f32[3,3,1,1,2048]{4,0,3,2,1:T(4,128)S(1)} %pad_maximum_fusion.12), channel_id=1, source_target_pairs={{8,0},{16,8},{24,16},{0,24},{9,1},{17,9},{25,17},{1,25},{10,2},{18... | collective-permute-start | bytes 221192 | tf_op jit(solution)/shard_map/ppermute | solution.py:28
  74.2 4.6 %collective-permute-start.20 = (f32[3,3,1,1,2048]{4,0,3,2,1:T(4,128)S(1)}, f32[3,3,1,1,2048]{4,0,3,2,1:T(4,128)S(1)}, u32[]{:S(2)}, u32[]{:S(2)}) collective-permute-start(f32[3,3,1,1,2048]{4,0,3,2,1:T(4,128)S(1)} %pad_maximum_fusion.12), channel_id=1, source_target_pairs={{0,8},{8,16},{16,24},{24,0},{1,9},{9,17},{17,25},{25,1},{2,10},{10... | collective-permute-start | bytes 221192 | tf_op jit(solution)/shard_map/ppermute | solution.py:26
  78.9 6.8 %collective-permute-start.23 = (f32[3,3,3,1,2048]{4,0,3,2,1:T(4,128)S(1)}, f32[3,3,3,1,2048]{4,0,3,2,1:T(4,128)S(1)}, u32[]{:S(2)}, u32[]{:S(2)}) collective-permute-start(f32[3,3,3,1,2048]{4,0,3,2,1:T(4,128)S(1)} %pad_maximum_fusion.7), channel_id=1, source_target_pairs={{1,0},{2,1},{3,2},{4,3},{5,4},{6,5},{7,6},{0,7},{9,8},{10,9},{11,1... | collective-permute-start | bytes 663560 | tf_op jit(solution)/shard_map/ppermute | solution.py:28
  79.5 7.9 %collective-permute-start.22 = (f32[3,3,3,1,2048]{4,0,3,2,1:T(4,128)S(1)}, f32[3,3,3,1,2048]{4,0,3,2,1:T(4,128)S(1)}, u32[]{:S(2)}, u32[]{:S(2)}) collective-permute-start(f32[3,3,3,1,2048]{4,0,3,2,1:T(4,128)S(1)} %pad_maximum_fusion.7), channel_id=1, source_target_pairs={{0,1},{1,2},{2,3},{3,4},{4,5},{5,6},{6,7},{7,0},{8,9},{9,10},{10,1... | collective-permute-start | bytes 663560 | tf_op jit(solution)/shard_map/ppermute | solution.py:26
where the time goes:
time: 136 us; the launch traced here: 135 us
  waiting for transfers between devices  41.2 us (30%)
  blocking collectives  38.3 us (28%)
  starting transfers between devices  32.8 us (24%)
  other arithmetic  12.4 us (9%)
  between operations  5.59 us (4%)
  local copies, waits for them, and re-layouts  5.09 us (4%)
    pmax x4, blocking collectives, one_axis_at_a_time(): value = lax.pmax(value, axis)  38.3 us
    ppermute x12, starting transfers between devices, with_halo(): lax.ppermute(head, axis, [((i + 1) % count, i) for i in range(count)])  27 us
    ppermute x12, waiting for transfers between devices, with_halo(): lax.ppermute(tail, axis, [(i, (i + 1) % count) for i in range(count)])  24.6 us
    ppermute x12, waiting for transfers between devices, with_halo(): lax.ppermute(head, axis, [((i + 1) % count, i) for i in range(count)])  16.6 us
    ppermute x12, starting transfers between devices, with_halo(): lax.ppermute(tail, axis, [(i, (i + 1) % count) for i in range(count)])  5.76 us
  transfers between devices with their start and end apart: 24, of which 18 were waited for; matrix products, arithmetic and copies ran while one was open for 4% of the time, Pallas kernels for 0%

commit v1 on v0

v1 whole, which is shorter than its diff:
```python
import jax
import jax.numpy as jnp
from jax import lax
from jax.sharding import PartitionSpec as P

ATOMS_DEV = 20480
BOUND = 2048
CROSS_BONDS = 4096
ITERS = 3
LOCAL_BONDS = 20320
LANES = 128
CHAINS = ATOMS_DEV // LANES
RIM_CHAINS = BOUND // LANES
GROUPS = CROSS_BONDS // BOUND
AXES = ("gx", "gy", "gz")
WEIGHT = {"gx": 9, "gy": 3, "gz": 1}
ORDER = ("gx", "gy", "gz")

relax_factor = 0.7


def partners(count):
    first = [(i, i ^ 1) for i in range(count)]
    second = [(i, (i + 1) % count if i % 2 else (i - 1) % count) for i in range(count)]
    return first, second


def swap_both(first_send, second_send, axis):
    first, second = partners(lax.axis_size(axis))
    return lax.ppermute(first_send, axis, first), lax.ppermute(second_send, axis, second)


def dot(left, right):
    return left[0] * right[0] + left[1] * right[1] + left[2] * right[2]


def bond_numbers(rest, rest_sq, now, inverse_sum):
    excess = dot(now, now) - rest_sq
    deviation = jnp.abs(excess) / (2.0 * jnp.maximum(rest_sq, 1.0))
    factor = relax_factor * excess / (2.0 * inverse_sum * jnp.maximum(dot(rest, now), 1.0))
    return factor, deviation


def next_atom(values):
    return jnp.roll(values, -1, axis=-1)


def chain_step(anchor, inverse, current):
    lane = lax.broadcasted_iota(jnp.int32, inverse.shape, 1)
    inside = lane < LANES - 1
    rest = [a - next_atom(a) for a in anchor]
    now = [c - next_atom(c) for c in current]
    factor, deviation = bond_numbers(rest, dot(rest, rest), now, inverse + next_atom(inverse))
    factor = jnp.where(inside, factor, 0.0)
    terms = [factor * r for r in rest]
    delta = [(jnp.roll(t, 1, axis=-1) - t) * inverse for t in terms]
    return delta, jnp.where(inside, deviation, 0.0)


def pick(blocks, index):
    picked = blocks[0]
    for number in range(1, 9):
        picked = jnp.where(index == number, blocks[number], picked)
    return picked


def local(ref_pos, step, inv_mass, boundary, bonds):
    anchor = ref_pos[0, 0, 0].reshape(3, CHAINS, LANES)
    moved = anchor + step[0, 0, 0].reshape(3, CHAINS, LANES)
    inverse = inv_mass[0, 0, 0].reshape(CHAINS, LANES)
    first_chain = boundary[0, 0, 0, 0] // LANES

    def rim(values):
        return lax.dynamic_slice_in_dim(values, first_chain, RIM_CHAINS, values.ndim - 2)

    sign = {a: 1 - 2 * (lax.axis_index(a) % 2) for a in AXES}
    offsets = {a: (sign[a], 0, -sign[a]) for a in AXES}
    ids = ((bonds[0, 0, 0, 1, LOCAL_BONDS:] - ATOMS_DEV) // BOUND).reshape(GROUPS, RIM_CHAINS, LANES)
    parts = {"gx": ids // 9 - 1, "gy": ids // 3 % 3 - 1, "gz": ids % 3 - 1}
    place = {a: 1 - parts[a] * sign[a] for a in AXES}
    s0, s1, s2 = ORDER
    spot = place[s1] * 3 + place[s0]
    plane = place[s2]
    both = plane[0] == plane[1]
    use_last = jnp.stack([both & (spot[1] < spot[0]), both & (spot[0] < spot[1])])

    rim_anchor = rim(anchor)
    rim_inverse = rim(inverse)
    rim_moved = rim(moved)

    def columns(values):
        one, two = swap_both(values, values, s0)
        row = jnp.stack([one, values, two])
        one, two = swap_both(row, row, s1)
        return [b[i] for b in (one, row, two) for i in range(3)]

    def gather(blocks, tables):
        first_send = jnp.stack([pick(blocks, tables[0][0]), pick(blocks, tables[0][1])])
        second_send = jnp.stack([pick(blocks, tables[1][0]), pick(blocks, tables[1][1])])
        one, two = swap_both(first_send, second_send, s2)
        far = []
        for group in range(GROUPS):
            last = use_last[group]
            here = pick(blocks, spot[group])
            from_one = jnp.where(last, one[1], one[0])
            from_two = jnp.where(last, two[1], two[0])
            far.append(
                jnp.where(plane[group] == 1, here, jnp.where(plane[group] == 0, from_one, from_two))
            )
        return far

    payload = jnp.concatenate(
        [rim_anchor, rim_moved, rim_inverse[None], ids.astype(jnp.float32)], axis=0
    )
    blocks = columns(payload)

    def wanted(toward):
        first_spot = jnp.full((RIM_CHAINS, LANES), 9, jnp.int32)
        last_spot = jnp.full((RIM_CHAINS, LANES), -1, jnp.int32)
        for number in range(9):
            back0 = offsets[s0][number % 3]
            back1 = offsets[s1][number // 3]
            code = 13 - back0 * WEIGHT[s0] - back1 * WEIGHT[s1] + toward * WEIGHT[s2]
            code = jnp.asarray(code, jnp.float32)
            found = (blocks[number][7] == code) | (blocks[number][8] == code)
            first_spot = jnp.minimum(first_spot, jnp.where(found, number, 9))
            last_spot = jnp.maximum(last_spot, jnp.where(found, number, -1))
        return first_spot, last_spot

    tables = (wanted(offsets[s2][0]), wanted(offsets[s2][2]))
    far = gather([b[:7] for b in blocks], tables)
    cross_rest = [[rim_anchor[i] - far[g][i] for i in range(3)] for g in range(GROUPS)]
    cross_sq = [dot(cross_rest[g], cross_rest[g]) for g in range(GROUPS)]
    cross_inverse = [rim_inverse + far[g][6] for g in range(GROUPS)]
    far_moved = [far[g][3:6] for g in range(GROUPS)]

    chain = lax.broadcasted_iota(jnp.int32, (CHAINS, LANES), 0)
    outside = (chain < first_chain) | (chain >= first_chain + RIM_CHAINS)
    body = [moved[i] for i in range(3)]
    edge = [rim_moved[i] for i in range(3)]
    reports = []
    for iteration in range(ITERS):
        delta, deviation = chain_step([anchor[i] for i in range(3)], inverse, body)
        body = [b + d for b, d in zip(body, delta)]
        body_worst = jnp.max(jnp.where(outside, deviation, 0.0))

        if iteration > 0:
            far_moved = gather(columns(jnp.stack(edge)), tables)
        delta, rim_dev = chain_step([rim_anchor[i] for i in range(3)], rim_inverse, edge)
        shift = [jnp.zeros((RIM_CHAINS, LANES), jnp.float32)] * 3
        for group in range(GROUPS):
            now = [edge[i] - far_moved[group][i] for i in range(3)]
            factor, deviation = bond_numbers(
                cross_rest[group], cross_sq[group], now, cross_inverse[group]
            )
            shift = [s + factor * r for s, r in zip(shift, cross_rest[group])]
            rim_dev = jnp.maximum(rim_dev, deviation)
        edge = [e + d - s * rim_inverse for e, d, s in zip(edge, delta, shift)]
        reports.append(jnp.maximum(body_worst, jnp.max(rim_dev)))

    positions = lax.dynamic_update_slice_in_dim(jnp.stack(body), jnp.stack(edge), first_chain, 1)

    devices = 1
    for a in AXES:
        devices *= lax.axis_size(a)
    lane = lax.broadcasted_iota(jnp.int32, (devices, LANES), 1)
    row = jnp.where(lane == 0, reports[0], jnp.where(lane == 1, reports[1], reports[2]))
    seen = lax.all_to_all(row, AXES, 0, 0, tiled=True)
    summary = jnp.max(seen, axis=0)[:ITERS]
    return positions.reshape(1, 1, 1, 3, ATOMS_DEV), summary


def solution(mesh):
    placed = (
        P("gx", "gy", "gz", None, None),
        P("gx", "gy", "gz", None, None),
        P("gx", "gy", "gz", None),
        P("gx", "gy", "gz", None),
        P("gx", "gy", "gz", None, None),
    )
    return jax.shard_map(
        local,
        mesh=mesh,
        in_specs=placed,
        out_specs=(P("gx", "gy", "gz", None, None), P()),
        check_vma=False,
    )
```

time: 136 us -> 104 us (0.76)
  the two profiles are of different devices: /device:TPU:8 before, /device:TPU:1 now
where the time goes in v1:
time: 104 us
  starting transfers between devices  45.2 us (43%)
  waiting for transfers between devices  26.5 us (25%)
  other arithmetic  14.7 us (14%)
  local copies, waits for them, and re-layouts  11.1 us (11%)
  between operations  6.42 us (6%)
    ppermute x9, starting transfers between devices, swap_both(): lax.ppermute(second_send, axis, second)  24.9 us
    all_to_all x1, starting transfers between devices, local(): seen = lax.all_to_all(row, AXES, 0, 0, tiled=True)  13.4 us
    all_to_all x1, waiting for transfers between devices, local(): seen = lax.all_to_all(row, AXES, 0, 0, tiled=True)  12.6 us
    ppermute x9, waiting for transfers between devices, swap_both(): lax.ppermute(second_send, axis, second)  7.97 us
    ppermute x9, starting transfers between devices, swap_both(): lax.ppermute(first_send, axis, first)  6.8 us
    ppermute x9, waiting for transfers between devices, swap_both(): lax.ppermute(first_send, axis, first)  5.92 us
    concatenate x20, local copies, waits for them, and re-layouts, next_atom(): return jnp.roll(values, -1, axis=-1)  5.08 us
    add x5, other arithmetic, local(): body = [b + d for b, d in zip(body, delta)]  2.45 us
  transfers between devices with their start and end apart: 19, of which 10 were waited for; matrix products, arithmetic and copies ran while one was open for 16% of the time, Pallas kernels for 0%

profile of v1, /device:TPU:1, one launch (start us, length us, event | category | flops | bytes accessed | tf_op | source)
XLA Modules:
  0.0 103.9 jit_solution(16181221447556560595)
XLA Ops:
  1.4 0.9 slice_add_fusion
  2.3 1.1 %add.500 = f32[3,160,128]{2,1,0:T(8,128)S(1)} add(f32[3,160,128]{2,1,0:T(8,128)} %bitcast.1011, f32[3,160,128]{2,1,0:T(8,128)} %bitcast.1021) | non-fusion elementwise | flops 61440 | bytes 737280 | tf_op jit(solution)/shard_map/add | solution.py:69
  3.5 0.7 fusion.35
  4.1 0.6 fusion.108
  4.8 2.6 %collective-permute-start.1 = (f32[9,16,128]{2,1,0:T(8,128)}, f32[9,16,128]{2,1,0:T(8,128)S(1)}, u32[]{:S(2)}, u32[]{:S(2)}) collective-permute-start(f32[9,16,128]{2,1,0:T(8,128)} %get-tuple-element.190), channel_id=1, source_target_pairs={{0,224},{32,64},{64,32},{96,128},{128,96},{160,192},{192,160},{224... | collective-permute-start | bytes 221192 | tf_op jit(solution)/shard_map/ppermute | solution.py:30
  7.4 1.1 %collective-permute-start = (f32[9,16,128]{2,1,0:T(8,128)}, f32[9,16,128]{2,1,0:T(8,128)S(1)}, u32[]{:S(2)}, u32[]{:S(2)}) collective-permute-start(f32[9,16,128]{2,1,0:T(8,128)} %get-tuple-element.190), channel_id=1, source_target_pairs={{0,32},{32,0},{64,96},{96,64},{128,160},{160,128},{192,224},{224,1... | collective-permute-start | bytes 221192 | tf_op jit(solution)/shard_map/ppermute | solution.py:30
  8.7 0.8 slice_bitcast_fusion.96
  9.4 0.7 slice_bitcast_fusion.95
  10.1 0.8 slice_bitcast_fusion.92
  10.9 0.7 slice_bitcast_fusion.91
  11.6 0.8 slice_bitcast_fusion.98
  12.4 0.7 slice_bitcast_fusion.97
  13.1 0.8 select_reduce_fusion.2
  14.3 0.7 slice_bitcast_fusion.88
  15.0 0.6 slice_bitcast_fusion.87
  17.2 0.8 select_reduce_fusion
  18.2 0.8 select_reduce_fusion.1
  19.4 0.8 compare_bitcast_fusion.9
  20.4 0.6 copy-done.9
  21.0 1.5 %fusion.2 = (f32[1,160,128]{2,1,0:T(8,128)S(1)}, f32[1,160,128]{2,1,0:T(8,128)S(1)}, f32[1,160,128]{2,1,0:T(8,128)S(1)}, f32[1,160,128]{2,1,0:T(8,128)S(1)}, f32...) fusion(f32[1,160,128]{2,1,0:T(8,128)S(1)} %bitcast.927, f32[1,160,127]{2,1,0:T(8,128)} %get-tuple-element.180, ...), kind=kLoop, calls=%fused_computation.21 | loop fusion | flops 839680 | bytes 1720448 | tf_op jit(solution)/shard_map/add | solution.py:144
  23.2 1.4 %collective-permute-start.3 = (f32[3,9,16,128]{3,2,1,0:T(8,128)S(1)}, f32[3,9,16,128]{3,2,1,0:T(8,128)S(1)}, u32[]{:S(2)}, u32[]{:S(2)}) collective-permute-start(f32[3,9,16,128]{3,2,1,0:T(8,128)S(1)} %pad_maximum_fusion.1), channel_id=1, source_target_pairs={{0,8},{8,0},{16,24},{24,16},{1,9},{9,1},{17,25},{25,17},{2,10},{10... | collective-permute-start | bytes 663560 | tf_op jit(solution)/shard_map/ppermute | solution.py:30
  24.6 1.9 %collective-permute-start.2 = (f32[3,9,16,128]{3,2,1,0:T(8,128)S(1)}, f32[3,9,16,128]{3,2,1,0:T(8,128)S(1)}, u32[]{:S(2)}, u32[]{:S(2)}) collective-permute-start(f32[3,9,16,128]{3,2,1,0:T(8,128)S(1)} %pad_maximum_fusion.1), channel_id=1, source_target_pairs={{0,24},{8,16},{16,8},{24,0},{1,25},{9,17},{17,9},{25,1},{2,26},{10... | collective-permute-start | bytes 663560 | tf_op jit(solution)/shard_map/ppermute | solution.py:30
  26.6 3.8 %collective-permute-done.3 = f32[3,9,16,128]{3,2,1,0:T(8,128)S(1)} collective-permute-done((f32[3,9,16,128]{3,2,1,0:T(8,128)S(1)}, f32[3,9,16,128]{3,2,1,0:T(8,128)S(1)}, u32[]{:S(2)}, u32[]{:S(2)}) %collective-permute-start.3) | collective-permute-done | bytes 221216 | tf_op jit(solution)/shard_map/ppermute | solution.py:30
  30.4 2.2 %collective-permute-done.2 = f32[3,9,16,128]{3,2,1,0:T(8,128)S(1)} collective-permute-done((f32[3,9,16,128]{3,2,1,0:T(8,128)S(1)}, f32[3,9,16,128]{3,2,1,0:T(8,128)S(1)}, u32[]{:S(2)}, u32[]{:S(2)}) %collective-permute-start.2) | collective-permute-done | bytes 221216 | tf_op jit(solution)/shard_map/ppermute | solution.py:30
  32.9 1.7 %collective-permute-start.4 = (f32[2,7,16,128]{3,2,1,0:T(8,128)S(1)}, f32[2,7,16,128]{3,2,1,0:T(8,128)S(1)}, u32[]{:S(2)}, u32[]{:S(2)}) collective-permute-start(f32[2,7,16,128]{3,2,1,0:T(8,128)S(1)} %pad_maximum_fusion.2), channel_id=1, source_target_pairs={{0,1},{1,0},{2,3},{3,2},{4,5},{5,4},{6,7},{7,6},{8,9},{9,8},{10,11... | collective-permute-start | bytes 344072 | tf_op jit(solution)/shard_map/ppermute | solution.py:30
  34.8 4.8 %collective-permute-start.5 = (f32[2,7,16,128]{3,2,1,0:T(8,128)S(1)}, f32[2,7,16,128]{3,2,1,0:T(8,128)S(1)}, u32[]{:S(2)}, u32[]{:S(2)}) collective-permute-start(f32[2,7,16,128]{3,2,1,0:T(8,128)S(1)} %pad_maximum_fusion.3), channel_id=1, source_target_pairs={{0,7},{1,2},{2,1},{3,4},{4,3},{5,6},{6,5},{7,0},{8,15},{9,10},{10,... | collective-permute-start | bytes 344072 | tf_op jit(solution)/shard_map/ppermute | solution.py:30
  40.1 1.6 %collective-permute-done.5 = f32[2,7,16,128]{3,2,1,0:T(8,128)S(1)} collective-permute-done((f32[2,7,16,128]{3,2,1,0:T(8,128)S(1)}, f32[2,7,16,128]{3,2,1,0:T(8,128)S(1)}, u32[]{:S(2)}, u32[]{:S(2)}) %collective-permute-start.5) | collective-permute-done | bytes 114720 | tf_op jit(solution)/shard_map/ppermute | solution.py:30
  42.0 0.7 maximum_reduce_fusion.2
  43.2 2.3 %collective-permute-start.7 = (f32[3,16,128]{2,1,0:T(8,128)S(1)}, f32[3,16,128]{2,1,0:T(8,128)S(1)}, u32[]{:S(2)}, u32[]{:S(2)}) collective-permute-start(f32[3,16,128]{2,1,0:T(8,128)S(1)} %get-tuple-element.194), channel_id=1, source_target_pairs={{0,224},{32,64},{64,32},{96,128},{128,96},{160,192},{192,160},{224... | collective-permute-start | bytes 73736 | tf_op jit(solution)/shard_map/ppermute | solution.py:30
  45.9 1.2 %collective-permute-done.7 = f32[3,16,128]{2,1,0:T(8,128)S(1)} collective-permute-done((f32[3,16,128]{2,1,0:T(8,128)S(1)}, f32[3,16,128]{2,1,0:T(8,128)S(1)}, u32[]{:S(2)}, u32[]{:S(2)}) %collective-permute-start.7) | collective-permute-done | bytes 24608 | tf_op jit(solution)/shard_map/ppermute | solution.py:30
  47.2 2.0 %collective-permute-start.8 = (f32[3,3,16,128]{3,2,1,0:T(8,128)S(1)}, f32[3,3,16,128]{3,2,1,0:T(8,128)S(1)}, u32[]{:S(2)}, u32[]{:S(2)}) collective-permute-start(f32[3,3,16,128]{3,2,1,0:T(8,128)S(1)} %pad_maximum_fusion.5), channel_id=1, source_target_pairs={{0,24},{8,16},{16,8},{24,0},{1,25},{9,17},{17,9},{25,1},{2,26},{10... | collective-permute-start | bytes 221192 | tf_op jit(solution)/shard_map/ppermute | solution.py:30
  49.3 1.1 %collective-permute-done.9 = f32[3,3,16,128]{3,2,1,0:T(8,128)S(1)} collective-permute-done((f32[3,3,16,128]{3,2,1,0:T(8,128)S(1)}, f32[3,3,16,128]{3,2,1,0:T(8,128)S(1)}, u32[]{:S(2)}, u32[]{:S(2)}) %collective-permute-start.9) | collective-permute-done | bytes 73760 | tf_op jit(solution)/shard_map/ppermute | solution.py:30
  50.4 1.3 %collective-permute-done.8 = f32[3,3,16,128]{3,2,1,0:T(8,128)S(1)} collective-permute-done((f32[3,3,16,128]{3,2,1,0:T(8,128)S(1)}, f32[3,3,16,128]{3,2,1,0:T(8,128)S(1)}, u32[]{:S(2)}, u32[]{:S(2)}) %collective-permute-start.8) | collective-permute-done | bytes 73760 | tf_op jit(solution)/shard_map/ppermute | solution.py:30
  51.9 3.2 %collective-permute-start.11 = (f32[2,3,16,128]{3,2,1,0:T(8,128)S(1)}, f32[2,3,16,128]{3,2,1,0:T(8,128)S(1)}, u32[]{:S(2)}, u32[]{:S(2)}) collective-permute-start(f32[2,3,16,128]{3,2,1,0:T(8,128)S(1)} %pad_maximum_fusion.9), channel_id=1, source_target_pairs={{0,7},{1,2},{2,1},{3,4},{4,3},{5,6},{6,5},{7,0},{8,15},{9,10},{10,... | collective-permute-start | bytes 147464 | tf_op jit(solution)/shard_map/ppermute | solution.py:30
  57.9 3.2 %collective-permute-start.13 = (f32[3,16,128]{2,1,0:T(8,128)S(1)}, f32[3,16,128]{2,1,0:T(8,128)S(1)}, u32[]{:S(2)}, u32[]{:S(2)}) collective-permute-start(f32[3,16,128]{2,1,0:T(8,128)S(1)} %get-tuple-element.192), channel_id=1, source_target_pairs={{0,224},{32,64},{64,32},{96,128},{128,96},{160,192},{192,160},{224... | collective-permute-start | bytes 73736 | tf_op jit(solution)/shard_map/ppermute | solution.py:30
  61.1 1.3 %collective-permute-start.12 = (f32[3,16,128]{2,1,0:T(8,128)S(1)}, f32[3,16,128]{2,1,0:T(8,128)S(1)}, u32[]{:S(2)}, u32[]{:S(2)}) collective-permute-start(f32[3,16,128]{2,1,0:T(8,128)S(1)} %get-tuple-element.192), channel_id=1, source_target_pairs={{0,32},{32,0},{64,96},{96,64},{128,160},{160,128},{192,224},{224,1... | collective-permute-start | bytes 73736 | tf_op jit(solution)/shard_map/ppermute | solution.py:30
  62.4 0.7 copy-done.10
  63.7 1.9 %collective-permute-start.14 = (f32[3,3,16,128]{3,2,1,0:T(8,128)S(1)}, f32[3,3,16,128]{3,2,1,0:T(8,128)S(1)}, u32[]{:S(2)}, u32[]{:S(2)}) collective-permute-start(f32[3,3,16,128]{3,2,1,0:T(8,128)S(1)} %pad_maximum_fusion.6), channel_id=1, source_target_pairs={{0,24},{8,16},{16,8},{24,0},{1,25},{9,17},{17,9},{25,1},{2,26},{10... | collective-permute-start | bytes 221192 | tf_op jit(solution)/shard_map/ppermute | solution.py:30
  65.6 0.9 collective-permute-done.15
  66.5 1.6 %collective-permute-done.14 = f32[3,3,16,128]{3,2,1,0:T(8,128)S(1)} collective-permute-done((f32[3,3,16,128]{3,2,1,0:T(8,128)S(1)}, f32[3,3,16,128]{3,2,1,0:T(8,128)S(1)}, u32[]{:S(2)}, u32[]{:S(2)}) %collective-permute-start.14) | collective-permute-done | bytes 73760 | tf_op jit(solution)/shard_map/ppermute | solution.py:30
  68.2 0.5 collective-permute-start.16
  68.8 3.0 %collective-permute-start.17 = (f32[2,3,16,128]{3,2,1,0:T(8,128)S(1)}, f32[2,3,16,128]{3,2,1,0:T(8,128)S(1)}, u32[]{:S(2)}, u32[]{:S(2)}) collective-permute-start(f32[2,3,16,128]{3,2,1,0:T(8,128)S(1)} %pad_maximum_fusion.11), channel_id=1, source_target_pairs={{0,7},{1,2},{2,1},{3,4},{4,3},{5,6},{6,5},{7,0},{8,15},{9,10},{10,... | collective-permute-start | bytes 147464 | tf_op jit(solution)/shard_map/ppermute | solution.py:30
  71.8 0.7 maximum_reduce_fusion.1
  74.2 0.7 maximum_reduce_fusion
  76.1 0.7 broadcast_select_fusion
  76.8 13.4 %all-to-all-start = ((f32[256,1,128]{2,1,0:T(1,128)}), f32[256,1,128]{2,1,0:T(1,128)S(1)}, u32[]{:S(2)}, u32[]{:S(2)}) async-start(f32[256,1,128]{2,1,0:T(1,128)} %broadcast_select_fusion), calls=%async_computation | async-start | bytes 262144 | tf_op jit(solution)/shard_map/all_to_all | solution.py:168
  90.7 12.6 %all-to-all-done = f32[256,1,128]{2,1,0:T(1,128)S(1)} async-done(((f32[256,1,128]{2,1,0:T(1,128)}), f32[256,1,128]{2,1,0:T(1,128)S(1)}, u32[]{:S(2)}, u32[]{:S(2)}) %all-to-all-start) | async-done | bytes 131104 | tf_op jit(solution)/shard_map/all_to_all | solution.py:168
  103.3 0.6 reduce_max.69
  (222 shorter events, 8.1 us)
Async XLA Ops:
  0.6 1.6 %copy-start = (f32[1,1,1,20480]{3,2,1,0:T(1,128)S(1)}, f32[1,1,1,20480]{3,2,1,0:T(1,128)}, u32[]{:S(2)}) copy-start(f32[1,1,1,20480]{3,2,1,0:T(1,128)} %param.7) | copy-start | bytes 245764
  4.8 18.4 %collective-permute-start.1 = (f32[9,16,128]{2,1,0:T(8,128)}, f32[9,16,128]{2,1,0:T(8,128)S(1)}, u32[]{:S(2)}, u32[]{:S(2)}) collective-permute-start(f32[9,16,128]{2,1,0:T(8,128)} %get-tuple-element.190), channel_id=1, source_target_pairs={{0,224},{32,64},{64,32},{96,128},{128,96},{160,192},{192,160},{224... | collective-permute-start | bytes 221192 | tf_op jit(solution)/shard_map/ppermute | solution.py:30
  7.4 15.8 %collective-permute-start = (f32[9,16,128]{2,1,0:T(8,128)}, f32[9,16,128]{2,1,0:T(8,128)S(1)}, u32[]{:S(2)}, u32[]{:S(2)}) collective-permute-start(f32[9,16,128]{2,1,0:T(8,128)} %get-tuple-element.190), channel_id=1, source_target_pairs={{0,32},{32,0},{64,96},{96,64},{128,160},{160,128},{192,224},{224,1... | collective-permute-start | bytes 221192 | tf_op jit(solution)/shard_map/ppermute | solution.py:30
  8.5 9.7 %copy-start.8 = (pred[128]{0:T(512)(128)(4,1)}, pred[128]{0:T(512)(128)(4,1)S(1)}, u32[]{:S(2)}) copy-start(pred[128]{0:T(512)(128)(4,1)S(1)} %iota_compare_fusion.1) | copy-start | bytes 388
  20.2 21.5 %copy-start.23 = (pred[16,128]{1,0:T(8,128)(4,1)}, pred[16,128]{1,0:T(8,128)(4,1)S(1)}, u32[]{:S(2)}) copy-start(pred[16,128]{1,0:T(8,128)(4,1)S(1)} %get-tuple-element.195) | copy-start | bytes 6148
  20.2 21.5 %copy-start.25 = (pred[16,128]{1,0:T(8,128)(4,1)}, pred[16,128]{1,0:T(8,128)(4,1)S(1)}, u32[]{:S(2)}) copy-start(pred[16,128]{1,0:T(8,128)(4,1)S(1)} %get-tuple-element.197) | copy-start | bytes 6148
  20.2 21.5 %copy-start.27 = (pred[16,128]{1,0:T(8,128)(4,1)}, pred[16,128]{1,0:T(8,128)(4,1)S(1)}, u32[]{:S(2)}) copy-start(pred[16,128]{1,0:T(8,128)(4,1)S(1)} %get-tuple-element.200) | copy-start | bytes 6148
  20.2 21.5 %copy-start.29 = (pred[16,128]{1,0:T(8,128)(4,1)}, pred[16,128]{1,0:T(8,128)(4,1)S(1)}, u32[]{:S(2)}) copy-start(pred[16,128]{1,0:T(8,128)(4,1)S(1)} %get-tuple-element.201) | copy-start | bytes 6148
  20.2 21.5 %copy-start.31 = (pred[16,128]{1,0:T(8,128)(4,1)}, pred[16,128]{1,0:T(8,128)(4,1)S(1)}, u32[]{:S(2)}) copy-start(pred[16,128]{1,0:T(8,128)(4,1)S(1)} %get-tuple-element.202) | copy-start | bytes 6148
  20.2 21.5 %copy-start.33 = (pred[16,128]{1,0:T(8,128)(4,1)}, pred[16,128]{1,0:T(8,128)(4,1)S(1)}, u32[]{:S(2)}) copy-start(pred[16,128]{1,0:T(8,128)(4,1)S(1)} %get-tuple-element.203) | copy-start | bytes 6148
  20.2 21.5 %copy-start.35 = (pred[16,128]{1,0:T(8,128)(4,1)}, pred[16,128]{1,0:T(8,128)(4,1)S(1)}, u32[]{:S(2)}) copy-start(pred[16,128]{1,0:T(8,128)(4,1)S(1)} %get-tuple-element.204) | copy-start | bytes 6148
  20.2 21.5 %copy-start.37 = (pred[16,128]{1,0:T(8,128)(4,1)}, pred[16,128]{1,0:T(8,128)(4,1)S(1)}, u32[]{:S(2)}) copy-start(pred[16,128]{1,0:T(8,128)(4,1)S(1)} %get-tuple-element.205) | copy-start | bytes 6148
  20.3 21.5 %copy-start.39 = (pred[16,128]{1,0:T(8,128)(4,1)}, pred[16,128]{1,0:T(8,128)(4,1)S(1)}, u32[]{:S(2)}) copy-start(pred[16,128]{1,0:T(8,128)(4,1)S(1)} %get-tuple-element.206) | copy-start | bytes 6148
  20.3 21.5 %copy-start.41 = (pred[16,128]{1,0:T(8,128)(4,1)}, pred[16,128]{1,0:T(8,128)(4,1)S(1)}, u32[]{:S(2)}) copy-start(pred[16,128]{1,0:T(8,128)(4,1)S(1)} %get-tuple-element.207) | copy-start | bytes 6148
  20.3 21.6 %copy-start.11 = (pred[16,128]{1,0:T(8,128)(4,1)}, pred[16,128]{1,0:T(8,128)(4,1)S(1)}, u32[]{:S(2)}) copy-start(pred[16,128]{1,0:T(8,128)(4,1)S(1)} %get-tuple-element.196) | copy-start | bytes 6148
  20.3 21.6 %copy-start.13 = (pred[16,128]{1,0:T(8,128)(4,1)}, pred[16,128]{1,0:T(8,128)(4,1)S(1)}, u32[]{:S(2)}) copy-start(pred[16,128]{1,0:T(8,128)(4,1)S(1)} %get-tuple-element.198) | copy-start | bytes 6148
  20.3 21.6 %copy-start.15 = (pred[16,128]{1,0:T(8,128)(4,1)}, pred[16,128]{1,0:T(8,128)(4,1)S(1)}, u32[]{:S(2)}) copy-start(pred[16,128]{1,0:T(8,128)(4,1)S(1)} %get-tuple-element.208) | copy-start | bytes 6148
  20.3 21.6 %copy-start.17 = (pred[16,128]{1,0:T(8,128)(4,1)}, pred[16,128]{1,0:T(8,128)(4,1)S(1)}, u32[]{:S(2)}) copy-start(pred[16,128]{1,0:T(8,128)(4,1)S(1)} %get-tuple-element.209) | copy-start | bytes 6148
  20.3 21.6 %copy-start.19 = (pred[16,128]{1,0:T(8,128)(4,1)}, pred[16,128]{1,0:T(8,128)(4,1)S(1)}, u32[]{:S(2)}) copy-start(pred[16,128]{1,0:T(8,128)(4,1)S(1)} %get-tuple-element.210) | copy-start | bytes 6148
  20.3 21.6 %copy-start.21 = (pred[16,128]{1,0:T(8,128)(4,1)}, pred[16,128]{1,0:T(8,128)(4,1)S(1)}, u32[]{:S(2)}) copy-start(pred[16,128]{1,0:T(8,128)(4,1)S(1)} %get-tuple-element.211) | copy-start | bytes 6148
  23.2 3.3 %copy-start.6 = (s32[2,16,128]{2,1,0:T(8,128)S(1)}, s32[2,16,128]{2,1,0:T(8,128)}, u32[]{:S(2)}) copy-start(s32[2,16,128]{2,1,0:T(8,128)} %get-tuple-element.219) | copy-start | bytes 49156
  23.2 3.3 %copy-start.7 = (s32[2,16,128]{2,1,0:T(8,128)S(1)}, s32[2,16,128]{2,1,0:T(8,128)}, u32[]{:S(2)}) copy-start(s32[2,16,128]{2,1,0:T(8,128)} %get-tuple-element.217) | copy-start | bytes 49156
  23.2 7.1 %collective-permute-start.3 = (f32[3,9,16,128]{3,2,1,0:T(8,128)S(1)}, f32[3,9,16,128]{3,2,1,0:T(8,128)S(1)}, u32[]{:S(2)}, u32[]{:S(2)}) collective-permute-start(f32[3,9,16,128]{3,2,1,0:T(8,128)S(1)} %pad_maximum_fusion.1), channel_id=1, source_target_pairs={{0,8},{8,0},{16,24},{24,16},{1,9},{9,1},{17,25},{25,17},{2,10},{10... | collective-permute-start | bytes 663560 | tf_op jit(solution)/shard_map/ppermute | solution.py:30
  24.6 8.0 %collective-permute-start.2 = (f32[3,9,16,128]{3,2,1,0:T(8,128)S(1)}, f32[3,9,16,128]{3,2,1,0:T(8,128)S(1)}, u32[]{:S(2)}, u32[]{:S(2)}) collective-permute-start(f32[3,9,16,128]{3,2,1,0:T(8,128)S(1)} %pad_maximum_fusion.1), channel_id=1, source_target_pairs={{0,24},{8,16},{16,8},{24,0},{1,25},{9,17},{17,9},{25,1},{2,26},{10... | collective-permute-start | bytes 663560 | tf_op jit(solution)/shard_map/ppermute | solution.py:30
  26.5 6.0 %copy-start.4 = (f32[2,16,128]{2,1,0:T(8,128)S(1)}, f32[2,16,128]{2,1,0:T(8,128)}, u32[]{:S(2)}) copy-start(f32[2,16,128]{2,1,0:T(8,128)} %copy-done.3) | copy-start | bytes 49156
  32.9 7.1 %collective-permute-start.4 = (f32[2,7,16,128]{3,2,1,0:T(8,128)S(1)}, f32[2,7,16,128]{3,2,1,0:T(8,128)S(1)}, u32[]{:S(2)}, u32[]{:S(2)}) collective-permute-start(f32[2,7,16,128]{3,2,1,0:T(8,128)S(1)} %pad_maximum_fusion.2), channel_id=1, source_target_pairs={{0,1},{1,0},{2,3},{3,2},{4,5},{5,4},{6,7},{7,6},{8,9},{9,8},{10,11... | collective-permute-start | bytes 344072 | tf_op jit(solution)/shard_map/ppermute | solution.py:30
  34.8 6.9 %collective-permute-start.5 = (f32[2,7,16,128]{3,2,1,0:T(8,128)S(1)}, f32[2,7,16,128]{3,2,1,0:T(8,128)S(1)}, u32[]{:S(2)}, u32[]{:S(2)}) collective-permute-start(f32[2,7,16,128]{3,2,1,0:T(8,128)S(1)} %pad_maximum_fusion.3), channel_id=1, source_target_pairs={{0,7},{1,2},{2,1},{3,4},{4,3},{5,6},{6,5},{7,0},{8,15},{9,10},{10,... | collective-permute-start | bytes 344072 | tf_op jit(solution)/shard_map/ppermute | solution.py:30
  43.2 3.9 %collective-permute-start.7 = (f32[3,16,128]{2,1,0:T(8,128)S(1)}, f32[3,16,128]{2,1,0:T(8,128)S(1)}, u32[]{:S(2)}, u32[]{:S(2)}) collective-permute-start(f32[3,16,128]{2,1,0:T(8,128)S(1)} %get-tuple-element.194), channel_id=1, source_target_pairs={{0,224},{32,64},{64,32},{96,128},{128,96},{160,192},{192,160},{224... | collective-permute-start | bytes 73736 | tf_op jit(solution)/shard_map/ppermute | solution.py:30
  45.5 1.5 %collective-permute-start.6 = (f32[3,16,128]{2,1,0:T(8,128)S(1)}, f32[3,16,128]{2,1,0:T(8,128)S(1)}, u32[]{:S(2)}, u32[]{:S(2)}) collective-permute-start(f32[3,16,128]{2,1,0:T(8,128)S(1)} %get-tuple-element.194), channel_id=1, source_target_pairs={{0,32},{32,0},{64,96},{96,64},{128,160},{160,128},{192,224},{224,1... | collective-permute-start | bytes 73736 | tf_op jit(solution)/shard_map/ppermute | solution.py:30
  47.1 3.3 %collective-permute-start.9 = (f32[3,3,16,128]{3,2,1,0:T(8,128)S(1)}, f32[3,3,16,128]{3,2,1,0:T(8,128)S(1)}, u32[]{:S(2)}, u32[]{:S(2)}) collective-permute-start(f32[3,3,16,128]{3,2,1,0:T(8,128)S(1)} %pad_maximum_fusion.5), channel_id=1, source_target_pairs={{0,8},{8,0},{16,24},{24,16},{1,9},{9,1},{17,25},{25,17},{2,10},{10... | collective-permute-start | bytes 221192 | tf_op jit(solution)/shard_map/ppermute | solution.py:30
  47.2 4.5 %collective-permute-start.8 = (f32[3,3,16,128]{3,2,1,0:T(8,128)S(1)}, f32[3,3,16,128]{3,2,1,0:T(8,128)S(1)}, u32[]{:S(2)}, u32[]{:S(2)}) collective-permute-start(f32[3,3,16,128]{3,2,1,0:T(8,128)S(1)} %pad_maximum_fusion.5), channel_id=1, source_target_pairs={{0,24},{8,16},{16,8},{24,0},{1,25},{9,17},{17,9},{25,1},{2,26},{10... | collective-permute-start | bytes 221192 | tf_op jit(solution)/shard_map/ppermute | solution.py:30
  51.7 5.0 %collective-permute-start.10 = (f32[2,3,16,128]{3,2,1,0:T(8,128)S(1)}, f32[2,3,16,128]{3,2,1,0:T(8,128)S(1)}, u32[]{:S(2)}, u32[]{:S(2)}) collective-permute-start(f32[2,3,16,128]{3,2,1,0:T(8,128)S(1)} %pad_maximum_fusion.8), channel_id=1, source_target_pairs={{0,1},{1,0},{2,3},{3,2},{4,5},{5,4},{6,7},{7,6},{8,9},{9,8},{10,11... | collective-permute-start | bytes 147464 | tf_op jit(solution)/shard_map/ppermute | solution.py:30
  51.9 4.9 %collective-permute-start.11 = (f32[2,3,16,128]{3,2,1,0:T(8,128)S(1)}, f32[2,3,16,128]{3,2,1,0:T(8,128)S(1)}, u32[]{:S(2)}, u32[]{:S(2)}) collective-permute-start(f32[2,3,16,128]{3,2,1,0:T(8,128)S(1)} %pad_maximum_fusion.9), channel_id=1, source_target_pairs={{0,7},{1,2},{2,1},{3,4},{4,3},{5,6},{6,5},{7,0},{8,15},{9,10},{10,... | collective-permute-start | bytes 147464 | tf_op jit(solution)/shard_map/ppermute | solution.py:30
  55.2 1.6 %copy-start.30 = (pred[16,128]{1,0:T(8,128)(4,1)S(1)}, pred[16,128]{1,0:T(8,128)(4,1)}, u32[]{:S(2)}) copy-start(pred[16,128]{1,0:T(8,128)(4,1)} %copy-done.29) | copy-start | bytes 6148
  55.2 1.6 %copy-start.32 = (pred[16,128]{1,0:T(8,128)(4,1)S(1)}, pred[16,128]{1,0:T(8,128)(4,1)}, u32[]{:S(2)}) copy-start(pred[16,128]{1,0:T(8,128)(4,1)} %copy-done.31) | copy-start | bytes 6148
  55.2 1.6 %copy-start.34 = (pred[16,128]{1,0:T(8,128)(4,1)S(1)}, pred[16,128]{1,0:T(8,128)(4,1)}, u32[]{:S(2)}) copy-start(pred[16,128]{1,0:T(8,128)(4,1)} %copy-done.33) | copy-start | bytes 6148
  55.2 1.6 %copy-start.36 = (pred[16,128]{1,0:T(8,128)(4,1)S(1)}, pred[16,128]{1,0:T(8,128)(4,1)}, u32[]{:S(2)}) copy-start(pred[16,128]{1,0:T(8,128)(4,1)} %copy-done.35) | copy-start | bytes 6148
  55.2 1.6 %copy-start.38 = (pred[16,128]{1,0:T(8,128)(4,1)S(1)}, pred[16,128]{1,0:T(8,128)(4,1)}, u32[]{:S(2)}) copy-start(pred[16,128]{1,0:T(8,128)(4,1)} %copy-done.37) | copy-start | bytes 6148
  55.2 1.6 %copy-start.40 = (pred[16,128]{1,0:T(8,128)(4,1)S(1)}, pred[16,128]{1,0:T(8,128)(4,1)}, u32[]{:S(2)}) copy-start(pred[16,128]{1,0:T(8,128)(4,1)} %copy-done.39) | copy-start | bytes 6148
  55.2 1.6 %copy-start.42 = (pred[16,128]{1,0:T(8,128)(4,1)S(1)}, pred[16,128]{1,0:T(8,128)(4,1)}, u32[]{:S(2)}) copy-start(pred[16,128]{1,0:T(8,128)(4,1)} %copy-done.41) | copy-start | bytes 6148
  57.9 5.3 %collective-permute-start.13 = (f32[3,16,128]{2,1,0:T(8,128)S(1)}, f32[3,16,128]{2,1,0:T(8,128)S(1)}, u32[]{:S(2)}, u32[]{:S(2)}) collective-permute-start(f32[3,16,128]{2,1,0:T(8,128)S(1)} %get-tuple-element.192), channel_id=1, source_target_pairs={{0,224},{32,64},{64,32},{96,128},{128,96},{160,192},{192,160},{224... | collective-permute-start | bytes 73736 | tf_op jit(solution)/shard_map/ppermute | solution.py:30
  61.1 2.2 %collective-permute-start.12 = (f32[3,16,128]{2,1,0:T(8,128)S(1)}, f32[3,16,128]{2,1,0:T(8,128)S(1)}, u32[]{:S(2)}, u32[]{:S(2)}) collective-permute-start(f32[3,16,128]{2,1,0:T(8,128)S(1)} %get-tuple-element.192), channel_id=1, source_target_pairs={{0,32},{32,0},{64,96},{96,64},{128,160},{160,128},{192,224},{224,1... | collective-permute-start | bytes 73736 | tf_op jit(solution)/shard_map/ppermute | solution.py:30
  63.2 3.2 %collective-permute-start.15 = (f32[3,3,16,128]{3,2,1,0:T(8,128)S(1)}, f32[3,3,16,128]{3,2,1,0:T(8,128)S(1)}, u32[]{:S(2)}, u32[]{:S(2)}) collective-permute-start(f32[3,3,16,128]{3,2,1,0:T(8,128)S(1)} %pad_maximum_fusion.6), channel_id=1, source_target_pairs={{0,8},{8,0},{16,24},{24,16},{1,9},{9,1},{17,25},{25,17},{2,10},{10... | collective-permute-start | bytes 221192 | tf_op jit(solution)/shard_map/ppermute | solution.py:30
  63.7 4.4 %collective-permute-start.14 = (f32[3,3,16,128]{3,2,1,0:T(8,128)S(1)}, f32[3,3,16,128]{3,2,1,0:T(8,128)S(1)}, u32[]{:S(2)}, u32[]{:S(2)}) collective-permute-start(f32[3,3,16,128]{3,2,1,0:T(8,128)S(1)} %pad_maximum_fusion.6), channel_id=1, source_target_pairs={{0,24},{8,16},{16,8},{24,0},{1,25},{9,17},{17,9},{25,1},{2,26},{10... | collective-permute-start | bytes 221192 | tf_op jit(solution)/shard_map/ppermute | solution.py:30
  68.2 5.9 %collective-permute-start.16 = (f32[2,3,16,128]{3,2,1,0:T(8,128)S(1)}, f32[2,3,16,128]{3,2,1,0:T(8,128)S(1)}, u32[]{:S(2)}, u32[]{:S(2)}) collective-permute-start(f32[2,3,16,128]{3,2,1,0:T(8,128)S(1)} %pad_maximum_fusion.10), channel_id=1, source_target_pairs={{0,1},{1,0},{2,3},{3,2},{4,5},{5,4},{6,7},{7,6},{8,9},{9,8},{10,11... | collective-permute-start | bytes 147464 | tf_op jit(solution)/shard_map/ppermute | solution.py:30
  68.8 5.3 %collective-permute-start.17 = (f32[2,3,16,128]{3,2,1,0:T(8,128)S(1)}, f32[2,3,16,128]{3,2,1,0:T(8,128)S(1)}, u32[]{:S(2)}, u32[]{:S(2)}) collective-permute-start(f32[2,3,16,128]{3,2,1,0:T(8,128)S(1)} %pad_maximum_fusion.11), channel_id=1, source_target_pairs={{0,7},{1,2},{2,1},{3,4},{4,3},{5,6},{6,5},{7,0},{8,15},{9,10},{10,... | collective-permute-start | bytes 147464 | tf_op jit(solution)/shard_map/ppermute | solution.py:30
  76.8 26.5 %all-to-all-start = ((f32[256,1,128]{2,1,0:T(1,128)}), f32[256,1,128]{2,1,0:T(1,128)S(1)}, u32[]{:S(2)}, u32[]{:S(2)}) async-start(f32[256,1,128]{2,1,0:T(1,128)} %broadcast_select_fusion), calls=%async_computation | async-start | bytes 262144 | tf_op jit(solution)/shard_map/all_to_all | solution.py:168
  90.7 13.2 %copy-start.5 = (f32[3,160,128]{2,1,0:T(8,128)}, f32[3,160,128]{2,1,0:T(8,128)S(1)}, u32[]{:S(2)}) copy-start(f32[3,160,128]{2,1,0:T(8,128)S(1)} %dynamic_update_slice.3) | copy-start | bytes 737284
  (14 other events, 12.8 us)

commit v2 on v1

v2 whole, which is shorter than its diff:
```python
import jax
import jax.numpy as jnp
from jax import lax
from jax.experimental import pallas as pl
from jax.experimental.pallas import tpu as pltpu
from jax.sharding import PartitionSpec as P

ATOMS_DEV = 20480
BOUND = 2048
CROSS_BONDS = 4096
ITERS = 3
LOCAL_BONDS = 20320
LANES = 128
CHAINS = ATOMS_DEV // LANES
RIM_CHAINS = BOUND // LANES
GROUPS = CROSS_BONDS // BOUND
AXES = ("gx", "gy", "gz")
WEIGHT = {"gx": 9, "gy": 3, "gz": 1}
ORDER = ("gy", "gx", "gz")
SHIFTED = ("gy", "gz", )

relax_factor = 0.7


def partners(count):
    first = [(i, i ^ 1) for i in range(count)]
    second = [(i, (i + 1) % count if i % 2 else (i - 1) % count) for i in range(count)]
    return first, second


def swap_both(first_send, second_send, axis):
    count = lax.axis_size(axis)
    if axis in SHIFTED:
        first = [(i, (i + 1) % count) for i in range(count)]
        second = [((i + 1) % count, i) for i in range(count)]
    else:
        first, second = partners(count)
    return lax.ppermute(first_send, axis, first), lax.ppermute(second_send, axis, second)


def dot(left, right):
    return left[0] * right[0] + left[1] * right[1] + left[2] * right[2]


def bond_numbers(rest, rest_sq, now, inverse_sum):
    excess = dot(now, now) - rest_sq
    deviation = jnp.abs(excess) / (2.0 * jnp.maximum(rest_sq, 1.0))
    factor = relax_factor * excess / (2.0 * inverse_sum * jnp.maximum(dot(rest, now), 1.0))
    return factor, deviation


def near(values):
    return pltpu.with_memory_space_constraint(values, pltpu.VMEM)


def next_atom(values):
    return pltpu.roll(values, LANES - 1, 1)


def chain_shift(factor, rest, inverse):
    terms = [factor * r for r in rest]
    return [(pltpu.roll(t, 1, 1) - t) * inverse for t in terms]


def fold(values):
    return jnp.maximum(values[:8], values[8:])


def body_kernel(place_ref, anchor_ref, step_ref, inverse_ref, out_ref, worst_ref):
    inside = lax.broadcasted_iota(jnp.int32, (8, LANES), 1) < LANES - 1
    rim_block = place_ref[0] * (RIM_CHAINS // 8)

    def block(number, worst):
        rows = pl.ds(pl.multiple_of(number * 8, 8), 8)
        anchor = [anchor_ref[i, rows, :] for i in range(3)]
        current = [anchor[i] + step_ref[i, rows, :] for i in range(3)]
        inverse = inverse_ref[rows, :]
        counted = (number < rim_block) | (number >= rim_block + RIM_CHAINS // 8)
        rest = [a - next_atom(a) for a in anchor]
        rest_sq = dot(rest, rest)
        inverse_sum = inverse + next_atom(inverse)
        found = []
        for iteration in range(ITERS):
            now = [c - next_atom(c) for c in current]
            factor, deviation = bond_numbers(rest, rest_sq, now, inverse_sum)
            factor = jnp.where(inside, factor, 0.0)
            delta = chain_shift(factor, rest, inverse)
            current = [c + d for c, d in zip(current, delta)]
            found.append(jnp.maximum(worst[iteration], jnp.where(inside & counted, deviation, 0.0)))
        for i in range(3):
            out_ref[i, rows, :] = current[i]
        return tuple(found)

    zero = jnp.zeros((8, LANES), jnp.float32)
    worst = lax.fori_loop(0, CHAINS // 8, block, (zero,) * ITERS, unroll=4)
    for iteration in range(ITERS):
        worst_ref[iteration] = worst[iteration]


def run_body(place, anchor, step, inverse):
    smem = pl.BlockSpec(memory_space=pltpu.SMEM)
    vmem = pl.BlockSpec(memory_space=pltpu.VMEM)
    return pl.pallas_call(
        body_kernel,
        in_specs=[smem, vmem, vmem, vmem],
        out_specs=[vmem, vmem],
        out_shape=[
            pltpu.VMEM((3, CHAINS, LANES), jnp.float32),
            pltpu.VMEM((ITERS, 8, LANES), jnp.float32),
        ],
        cost_estimate=pl.CostEstimate(flops=6000000, transcendentals=0, bytes_accessed=900000),
        name="body",
    )(place, near(anchor), near(step), near(inverse))


def load_kernel(place_ref, anchor_ref, step_ref, inverse_ref, bonds_ref, out_ref, rows_ref):
    start = LOCAL_BONDS // LANES * LANES
    tail = LOCAL_BONDS - start
    rows = CROSS_BONDS // LANES
    for row in range(rows):
        rows_ref[row : row + 1, :] = bonds_ref[1:2, start + row * LANES : start + (row + 1) * LANES]
    rows_ref[rows : rows + 1, :tail] = bonds_ref[1:2, start + rows * LANES :]
    head = pltpu.roll(rows_ref[:rows, :], LANES - tail, 1)
    rest = pltpu.roll(rows_ref[1 : rows + 1, :], LANES - tail, 1)
    lane = lax.broadcasted_iota(jnp.int32, (rows, LANES), 1)
    ids = ((jnp.where(lane < LANES - tail, head, rest) - ATOMS_DEV) // BOUND).astype(jnp.float32)
    for i in range(3):
        out_ref[i] = anchor_ref[i]
        out_ref[3 + i] = anchor_ref[i] + step_ref[i]
    out_ref[6] = inverse_ref[...]
    for group in range(GROUPS):
        out_ref[7 + group] = ids[group * RIM_CHAINS : (group + 1) * RIM_CHAINS]


def run_load(place, anchor, step, inverse, bonds):
    rim3 = pl.BlockSpec((3, RIM_CHAINS, LANES), lambda i, place: (0, place[0], 0))
    rim1 = pl.BlockSpec((RIM_CHAINS, LANES), lambda i, place: (place[0], 0))
    whole = pl.BlockSpec(bonds.shape, lambda i, place: (0, 0))
    return pl.pallas_call(
        load_kernel,
        grid_spec=pltpu.PrefetchScalarGridSpec(
            num_scalar_prefetch=1,
            grid=(1,),
            in_specs=[rim3, rim3, rim1, whole],
            out_specs=pl.BlockSpec((9, RIM_CHAINS, LANES), lambda i, place: (0, 0, 0)),
            scratch_shapes=[pltpu.VMEM((CROSS_BONDS // LANES + 8, LANES), jnp.int32)],
        ),
        out_shape=pltpu.VMEM((9, RIM_CHAINS, LANES), jnp.float32),
        name="load",
    )(place, anchor, step, inverse, bonds)


def peak_kernel(seen_ref, out_ref):
    out_ref[...] = jnp.max(seen_ref[...], axis=0, keepdims=True)


def run_peak(seen):
    vmem = pl.BlockSpec(memory_space=pltpu.VMEM)
    return pl.pallas_call(
        peak_kernel,
        in_specs=[vmem],
        out_specs=vmem,
        out_shape=pltpu.VMEM((1, LANES), jnp.float32),
        name="peak",
    )(near(seen))


def edge_kernel(first, last, *refs):
    refs = list(refs)
    payload_ref = refs.pop(0)
    edge_ref = payload_ref if first else refs.pop(0)
    static_ref = None if first else refs.pop(0)
    one_ref, two_ref, here_ref, source_ref = [refs.pop(0) for _ in range(4)]
    lane = lax.broadcasted_iota(jnp.int32, (RIM_CHAINS, LANES), 1)
    inside = lane < LANES - 1
    anchor = [payload_ref[i] for i in range(3)]
    inverse = payload_ref[6]
    edge = [edge_ref[3 + i] if first else edge_ref[i] for i in range(3)]
    rest = [a - next_atom(a) for a in anchor]
    now = [c - next_atom(c) for c in edge]
    factor, deviation = bond_numbers(rest, dot(rest, rest), now, inverse + next_atom(inverse))
    delta = chain_shift(jnp.where(inside, factor, 0.0), rest, inverse)
    worst = jnp.where(inside, deviation, 0.0)
    shift = [0.0, 0.0, 0.0]
    kept = []
    for group in range(GROUPS):
        source = source_ref[group]

        def far(field):
            return jnp.where(
                source < 2,
                jnp.where(source == 0, one_ref[0, field], one_ref[1, field]),
                jnp.where(
                    source == 4,
                    here_ref[group, field],
                    jnp.where(source == 2, two_ref[0, field], two_ref[1, field]),
                ),
            )

        if first:
            far_anchor = [far(i) for i in range(3)]
            far_moved = [far(3 + i) for i in range(3)]
            far_inverse = far(6)
            kept.append(far_anchor + [far_inverse])
        else:
            far_anchor = [static_ref[group, i] for i in range(3)]
            far_inverse = static_ref[group, 3]
            far_moved = [far(i) for i in range(3)]
        rest = [a - f for a, f in zip(anchor, far_anchor)]
        now = [c - f for c, f in zip(edge, far_moved)]
        factor, deviation = bond_numbers(rest, dot(rest, rest), now, inverse + far_inverse)
        shift = [s + factor * r for s, r in zip(shift, rest)]
        worst = jnp.maximum(worst, deviation)
    edge = [e + d - s * inverse for e, d, s in zip(edge, delta, shift)]
    if last:
        worst_body_ref, worst0_ref, worst1_ref, out_ref, row_ref = refs
        found = []
        for iteration, rim in enumerate((worst0_ref[...], worst1_ref[...], fold(worst))):
            found.append(jnp.max(jnp.maximum(worst_body_ref[iteration], rim)))
        lane = lax.broadcasted_iota(jnp.int32, row_ref.shape, 1)
        row_ref[...] = jnp.where(lane == 0, found[0], jnp.where(lane == 1, found[1], found[2]))
    elif first:
        out_ref, worst_ref, kept_ref = refs
        worst_ref[...] = fold(worst)
        for group in range(GROUPS):
            for field in range(4):
                kept_ref[group, field] = kept[group][field]
    else:
        out_ref, worst_ref = refs
        worst_ref[...] = fold(worst)
    for i in range(3):
        out_ref[i] = edge[i]


def run_edge(first, last, devices, *operands):
    vmem = pl.BlockSpec(memory_space=pltpu.VMEM)
    shapes = [(3, RIM_CHAINS, LANES)]
    shapes.append((devices, LANES) if last else (8, LANES))
    if first:
        shapes.append((GROUPS, 4, RIM_CHAINS, LANES))
    return pl.pallas_call(
        lambda *refs: edge_kernel(first, last, *refs),
        in_specs=[vmem] * len(operands),
        out_specs=[vmem] * len(shapes),
        out_shape=[pltpu.VMEM(s, jnp.float32) for s in shapes],
        name="edge",
    )(*[near(operand) for operand in operands])


def pick(blocks, index):
    picked = blocks[0]
    for number in range(1, 9):
        picked = jnp.where(index == number, blocks[number], picked)
    return picked


def local(ref_pos, step, inv_mass, boundary, bonds):
    anchor = ref_pos.reshape(3, CHAINS, LANES)
    step = step.reshape(3, CHAINS, LANES)
    inverse = inv_mass.reshape(CHAINS, LANES)
    place_rim = (boundary // BOUND).reshape(1)

    sign = {a: -1 if a in SHIFTED else 1 - 2 * (lax.axis_index(a) % 2) for a in AXES}
    offsets = {a: (sign[a], 0, -sign[a]) for a in AXES}
    payload = run_load(place_rim, anchor, step, inverse, bonds[0, 0, 0])
    ids = payload[7:].astype(jnp.int32)
    parts = {"gx": ids // 9 - 1, "gy": ids // 3 % 3 - 1, "gz": ids % 3 - 1}
    place = {a: 1 - parts[a] * sign[a] for a in AXES}
    s0, s1, s2 = ORDER
    spot = place[s1] * 3 + place[s0]
    plane = place[s2]
    both = plane[0] == plane[1]
    use_last = jnp.stack([both & (spot[1] < spot[0]), both & (spot[0] < spot[1])]).astype(jnp.int32)
    source = jnp.where(plane == 1, 4, plane + use_last)

    def columns(values):
        one, two = swap_both(values, values, s0)
        row = jnp.stack([one, values, two])
        one, two = swap_both(row, row, s1)
        return [b[i] for b in (one, row, two) for i in range(3)]

    def exchange(blocks, tables):
        first_send = jnp.stack([pick(blocks, tables[0][0]), pick(blocks, tables[0][1])])
        second_send = jnp.stack([pick(blocks, tables[1][0]), pick(blocks, tables[1][1])])
        one, two = swap_both(first_send, second_send, s2)
        return one, two, jnp.stack([pick(blocks, spot[0]), pick(blocks, spot[1])])

    blocks = columns(payload)

    def wanted(toward):
        first_spot = jnp.full((RIM_CHAINS, LANES), 9, jnp.int32)
        last_spot = jnp.full((RIM_CHAINS, LANES), -1, jnp.int32)
        for number in range(9):
            back0 = offsets[s0][number % 3]
            back1 = offsets[s1][number // 3]
            code = 13 - back0 * WEIGHT[s0] - back1 * WEIGHT[s1] + toward * WEIGHT[s2]
            code = jnp.asarray(code, jnp.float32)
            found = (blocks[number][7] == code) | (blocks[number][8] == code)
            first_spot = jnp.minimum(first_spot, jnp.where(found, number, 9))
            last_spot = jnp.maximum(last_spot, jnp.where(found, number, -1))
        return first_spot, last_spot

    turn = -1 if s2 in SHIFTED else 1
    tables = (wanted(turn * offsets[s2][0]), wanted(turn * offsets[s2][2]))
    body, worst_body = run_body(place_rim, anchor, step, inverse)
    devices = 1
    for a in AXES:
        devices *= lax.axis_size(a)

    one, two, here = exchange([b[:7] for b in blocks], tables)
    edge, worst0, kept = run_edge(True, False, devices, payload, one, two, here, source)
    one, two, here = exchange(columns(edge), tables)
    edge, worst1 = run_edge(False, False, devices, payload, edge, kept, one, two, here, source)
    one, two, here = exchange(columns(edge), tables)
    edge, row = run_edge(
        False, True, devices, payload, edge, kept, one, two, here, source, worst_body, worst0, worst1
    )
    seen = lax.all_to_all(row, AXES, 0, 0, tiled=True)
    positions = lax.dynamic_update_slice_in_dim(body, edge, place_rim[0] * RIM_CHAINS, 1)
    summary = run_peak(seen)[0, :ITERS]
    return positions.reshape(1, 1, 1, 3, ATOMS_DEV), summary


def solution(mesh):
    placed = (
        P("gx", "gy", "gz", None, None),
        P("gx", "gy", "gz", None, None),
        P("gx", "gy", "gz", None),
        P("gx", "gy", "gz", None),
        P("gx", "gy", "gz", None, None),
    )
    return jax.shard_map(
        local,
        mesh=mesh,
        in_specs=placed,
        out_specs=(P("gx", "gy", "gz", None, None), P()),
        check_vma=False,
    )
```

time: 104 us -> 83.3 us (0.80)
  other arithmetic: 14.7 us -> 0.96 us
  waiting for transfers between devices: 26.5 us -> 36.4 us
  local copies, waits for them, and re-layouts: 11.1 us -> 1.24 us
  starting transfers between devices: 45.2 us -> 38.1 us
  Pallas kernels: 0 us -> 4.86 us
  between operations: 6.42 us -> 1.62 us
    ppermute x9, starting transfers between devices: 24.9 us -> 15.3 us  [swap_both(): lax.ppermute(second_send, axis, second)]
    ppermute x9, starting transfers between devices: 6.8 us -> 14.3 us  [swap_both(): lax.ppermute(first_send, axis, first)]
    concatenate x38 -> x0, local copies, waits for them, and re-layouts: 7.19 us -> none  [the longest x20 5.08 us: next_atom(): return jnp.roll(values, -1, axis=-1)]
    ppermute x9, waiting for transfers between devices: 7.97 us -> 13.9 us  [swap_both(): lax.ppermute(second_send, axis, second)]
    reduce_max x7 -> x0, other arithmetic: 5.07 us -> none  [the longest x3 2.43 us: local(): body_worst = jnp.max(jnp.where(outside, deviation, 0.0))]
    all_to_all x1, starting transfers between devices: 13.4 us -> 8.49 us  [local(): seen = lax.all_to_all(row, AXES, 0, 0, tiled=True)]
    pallas_call x0 -> x6, Pallas kernels: none -> 4.86 us  [the longest x1 2.54 us: run_body(): pl.pallas_call(body_kernel, in_specs=[smem, vmem, vmem, vmem], out_specs=...]
    ppermute x9, waiting for transfers between devices: 5.92 us -> 10.2 us  [swap_both(): lax.ppermute(first_send, axis, first)]
  transfers between devices with their start and end apart: 19 -> 19, of which waited for: 10 -> 15; matrix products, arithmetic and copies ran while one was open for 16% -> 2% of each run, Pallas kernels for 0% -> 3%
where the time goes in v2:
time: 83.3 us; the launch traced here: 83.2 us
  starting transfers between devices  38.1 us (46%)
  waiting for transfers between devices  36.4 us (44%)
  Pallas kernels  4.86 us (6%)
  between operations  1.62 us (2%)
  local copies, waits for them, and re-layouts  1.24 us (1%)
  other arithmetic  0.96 us (1%)
    ppermute x9, starting transfers between devices, swap_both(): lax.ppermute(second_send, axis, second)  15.3 us
    ppermute x9, starting transfers between devices, swap_both(): lax.ppermute(first_send, axis, first)  14.3 us
    ppermute x9, waiting for transfers between devices, swap_both(): lax.ppermute(second_send, axis, second)  13.9 us
    all_to_all x1, waiting for transfers between devices, local(): seen = lax.all_to_all(row, AXES, 0, 0, tiled=True)  12.3 us
    ppermute x9, waiting for transfers between devices, swap_both(): lax.ppermute(first_send, axis, first)  10.2 us
    all_to_all x1, starting transfers between devices, local(): seen = lax.all_to_all(row, AXES, 0, 0, tiled=True)  8.49 us
    pallas_call x1, Pallas kernels, run_body(): pl.pallas_call(body_kernel, in_specs=[smem, vmem, vmem, vmem], out_specs=...  2.54 us
  transfers between devices with their start and end apart: 19, of which 15 were waited for; matrix products, arithmetic and copies ran while one was open for 2% of the time, Pallas kernels for 3%

profile of v2, /device:TPU:1, one launch (start us, length us, event | category | flops | bytes accessed | tf_op | source)
XLA Modules:
  0.0 83.2 jit_solution(9326314272268238886)
XLA Ops:
  1.3 1.1 %load.1.refs_0_ = f32[9,16,128]{2,1,0:T(8,128)S(1)} custom-call(s32[1]{0:T(128)} %bitcast.place_ref, f32[3,160,128]{2,1,0:T(8,128)} %bitcast.470, f32[3,160,128]{2,1,0:T(8,128)} %bitcast.472, f32[160,128]{1,0:T(8,128)} %bitcast.475, s32[2,24416]{1,0:T(2,128)} %bitcast.483), custom_call_target="tpu_custom_call" | custom-call | tf_op jit(solution)/shard_map/load/pallas_call | solution.py:139
  2.4 3.6 %collective-permute-start.1 = (f32[9,16,128]{2,1,0:T(8,128)S(1)}, f32[9,16,128]{2,1,0:T(8,128)S(1)}, u32[]{:S(2)}, u32[]{:S(2)}) collective-permute-start(f32[9,16,128]{2,1,0:T(8,128)S(1)} %load.1.refs_0_), channel_id=1, source_target_pairs={{8,0},{16,8},{24,16},{0,24},{9,1},{17,9},{25,17},{1,25},{10,2},{18... | collective-permute-start | bytes 221192 | tf_op jit(solution)/shard_map/ppermute | solution.py:38
  6.0 0.0 collective-permute-start
  6.2 1.2 %collective-permute-done.1 = f32[9,16,128]{2,1,0:T(8,128)S(1)} collective-permute-done((f32[9,16,128]{2,1,0:T(8,128)S(1)}, f32[9,16,128]{2,1,0:T(8,128)S(1)}, u32[]{:S(2)}, u32[]{:S(2)}) %collective-permute-start.1) | collective-permute-done | bytes 73760 | tf_op jit(solution)/shard_map/ppermute | solution.py:38
  7.4 3.0 %collective-permute-done = f32[9,16,128]{2,1,0:T(8,128)S(1)} collective-permute-done((f32[9,16,128]{2,1,0:T(8,128)S(1)}, f32[9,16,128]{2,1,0:T(8,128)S(1)}, u32[]{:S(2)}, u32[]{:S(2)}) %collective-permute-start) | collective-permute-done | bytes 73760 | tf_op jit(solution)/shard_map/ppermute | solution.py:38
  10.5 3.3 %collective-permute-start.3 = (f32[3,9,16,128]{3,2,1,0:T(8,128)S(1)}, f32[3,9,16,128]{3,2,1,0:T(8,128)S(1)}, u32[]{:S(2)}, u32[]{:S(2)}) collective-permute-start(f32[3,9,16,128]{3,2,1,0:T(8,128)S(1)} %pad_maximum_fusion), channel_id=1, source_target_pairs={{0,224},{32,64},{64,32},{96,128},{128,96},{160,192},{192,160},{224... | collective-permute-start | bytes 663560 | tf_op jit(solution)/shard_map/ppermute | solution.py:38
  13.8 3.9 %collective-permute-done.3 = f32[3,9,16,128]{3,2,1,0:T(8,128)S(1)} collective-permute-done((f32[3,9,16,128]{3,2,1,0:T(8,128)S(1)}, f32[3,9,16,128]{3,2,1,0:T(8,128)S(1)}, u32[]{:S(2)}, u32[]{:S(2)}) %collective-permute-start.3) | collective-permute-done | bytes 221216 | tf_op jit(solution)/shard_map/ppermute | solution.py:38
  17.9 0.1 select_bitcast_fusion.4
  17.9 0.1 select_bitcast_fusion.5
  18.0 1.7 %collective-permute-start.4 = (f32[2,7,16,128]{3,2,1,0:T(8,128)S(1)}, f32[2,7,16,128]{3,2,1,0:T(8,128)S(1)}, u32[]{:S(2)}, u32[]{:S(2)}) collective-permute-start(f32[2,7,16,128]{3,2,1,0:T(8,128)S(1)} %pad_maximum_fusion.1), channel_id=1, source_target_pairs={{0,1},{1,2},{2,3},{3,4},{4,5},{5,6},{6,7},{7,0},{8,9},{9,10},{10,1... | collective-permute-start | bytes 344072 | tf_op jit(solution)/shard_map/ppermute | solution.py:38
  19.7 0.1 select_bitcast_fusion.3
  19.8 4.0 %collective-permute-start.5 = (f32[2,7,16,128]{3,2,1,0:T(8,128)S(1)}, f32[2,7,16,128]{3,2,1,0:T(8,128)S(1)}, u32[]{:S(2)}, u32[]{:S(2)}) collective-permute-start(f32[2,7,16,128]{3,2,1,0:T(8,128)S(1)} %pad_maximum_fusion.2), channel_id=1, source_target_pairs={{1,0},{2,1},{3,2},{4,3},{5,4},{6,5},{7,6},{0,7},{9,8},{10,9},{11,1... | collective-permute-start | bytes 344072 | tf_op jit(solution)/shard_map/ppermute | solution.py:38
  23.9 0.1 select_bitcast_fusion
  24.0 1.9 %collective-permute-done.4.refs_1_ = f32[2,7,16,128]{3,2,1,0:T(8,128)S(1)} collective-permute-done((f32[2,7,16,128]{3,2,1,0:T(8,128)S(1)}, f32[2,7,16,128]{3,2,1,0:T(8,128)S(1)}, u32[]{:S(2)}, u32[]{:S(2)}) %collective-permute-start.4) | collective-permute-done | bytes 114720 | tf_op jit(solution)/shard_map/ppermute | solution.py:38
  25.8 0.0 collective-permute-done.5.refs_2_
  25.8 0.2 edge.3
  26.0 0.1 collective-permute-start.7
  26.1 1.5 %collective-permute-start.6 = (f32[3,16,128]{2,1,0:T(8,128)S(1)}, f32[3,16,128]{2,1,0:T(8,128)S(1)}, u32[]{:S(2)}, u32[]{:S(2)}) collective-permute-start(f32[3,16,128]{2,1,0:T(8,128)S(1)} %get-tuple-element.12.refs_1_), channel_id=1, source_target_pairs={{0,8},{8,16},{16,24},{24,0},{1,9},{9,17},{17,25},{25,1},{2,10},{10... | collective-permute-start | bytes 73736 | tf_op jit(solution)/shard_map/ppermute | solution.py:38
  27.5 1.2 %collective-permute-done.7 = f32[3,16,128]{2,1,0:T(8,128)S(1)} collective-permute-done((f32[3,16,128]{2,1,0:T(8,128)S(1)}, f32[3,16,128]{2,1,0:T(8,128)S(1)}, u32[]{:S(2)}, u32[]{:S(2)}) %collective-permute-start.7) | collective-permute-done | bytes 24608 | tf_op jit(solution)/shard_map/ppermute | solution.py:38
  28.8 1.3 %collective-permute-done.6 = f32[3,16,128]{2,1,0:T(8,128)S(1)} collective-permute-done((f32[3,16,128]{2,1,0:T(8,128)S(1)}, f32[3,16,128]{2,1,0:T(8,128)S(1)}, u32[]{:S(2)}, u32[]{:S(2)}) %collective-permute-start.6) | collective-permute-done | bytes 24608 | tf_op jit(solution)/shard_map/ppermute | solution.py:38
  30.1 3.6 %collective-permute-start.9 = (f32[3,3,16,128]{3,2,1,0:T(8,128)S(1)}, f32[3,3,16,128]{3,2,1,0:T(8,128)S(1)}, u32[]{:S(2)}, u32[]{:S(2)}) collective-permute-start(f32[3,3,16,128]{3,2,1,0:T(8,128)S(1)} %pad_maximum_fusion.4), channel_id=1, source_target_pairs={{0,32},{32,0},{64,96},{96,64},{128,160},{160,128},{192,224},{224,1... | collective-permute-start | bytes 221192 | tf_op jit(solution)/shard_map/ppermute | solution.py:38
  33.6 0.6 collective-permute-start.8
  34.3 0.3 collective-permute-done.9
  34.6 3.2 %collective-permute-done.8 = f32[3,3,16,128]{3,2,1,0:T(8,128)S(1)} collective-permute-done((f32[3,3,16,128]{3,2,1,0:T(8,128)S(1)}, f32[3,3,16,128]{3,2,1,0:T(8,128)S(1)}, u32[]{:S(2)}, u32[]{:S(2)}) %collective-permute-start.8) | collective-permute-done | bytes 73760 | tf_op jit(solution)/shard_map/ppermute | solution.py:38
  37.8 0.1 collective-permute-start.10
  37.9 3.2 %collective-permute-start.11 = (f32[2,3,16,128]{3,2,1,0:T(8,128)S(1)}, f32[2,3,16,128]{3,2,1,0:T(8,128)S(1)}, u32[]{:S(2)}, u32[]{:S(2)}) collective-permute-start(f32[2,3,16,128]{3,2,1,0:T(8,128)S(1)} %pad_maximum_fusion.7), channel_id=1, source_target_pairs={{1,0},{2,1},{3,2},{4,3},{5,4},{6,5},{7,6},{0,7},{9,8},{10,9},{11,1... | collective-permute-start | bytes 147464 | tf_op jit(solution)/shard_map/ppermute | solution.py:38
  41.2 0.0 copy-start.1
  41.3 0.0 copy-start
  41.3 1.2 %collective-permute-done.10.refs_3_ = f32[2,3,16,128]{3,2,1,0:T(8,128)S(1)} collective-permute-done((f32[2,3,16,128]{3,2,1,0:T(8,128)S(1)}, f32[2,3,16,128]{3,2,1,0:T(8,128)S(1)}, u32[]{:S(2)}, u32[]{:S(2)}) %collective-permute-start.10) | collective-permute-done | bytes 49184 | tf_op jit(solution)/shard_map/ppermute | solution.py:38
  42.5 0.2 edge.4
  42.7 0.0 copy-start.2
  42.7 0.1 collective-permute-start.13
  42.8 1.5 %collective-permute-start.12 = (f32[3,16,128]{2,1,0:T(8,128)S(1)}, f32[3,16,128]{2,1,0:T(8,128)S(1)}, u32[]{:S(2)}, u32[]{:S(2)}) collective-permute-start(f32[3,16,128]{2,1,0:T(8,128)S(1)} %get-tuple-element.14.refs_1_), channel_id=1, source_target_pairs={{0,8},{8,16},{16,24},{24,0},{1,9},{9,17},{17,25},{25,1},{2,10},{10... | collective-permute-start | bytes 73736 | tf_op jit(solution)/shard_map/ppermute | solution.py:38
  44.2 1.2 %collective-permute-done.13 = f32[3,16,128]{2,1,0:T(8,128)S(1)} collective-permute-done((f32[3,16,128]{2,1,0:T(8,128)S(1)}, f32[3,16,128]{2,1,0:T(8,128)S(1)}, u32[]{:S(2)}, u32[]{:S(2)}) %collective-permute-start.13) | collective-permute-done | bytes 24608 | tf_op jit(solution)/shard_map/ppermute | solution.py:38
  45.5 1.3 %collective-permute-done.12 = f32[3,16,128]{2,1,0:T(8,128)S(1)} collective-permute-done((f32[3,16,128]{2,1,0:T(8,128)S(1)}, f32[3,16,128]{2,1,0:T(8,128)S(1)}, u32[]{:S(2)}, u32[]{:S(2)}) %collective-permute-start.12) | collective-permute-done | bytes 24608 | tf_op jit(solution)/shard_map/ppermute | solution.py:38
  46.8 3.0 %collective-permute-start.15 = (f32[3,3,16,128]{3,2,1,0:T(8,128)S(1)}, f32[3,3,16,128]{3,2,1,0:T(8,128)S(1)}, u32[]{:S(2)}, u32[]{:S(2)}) collective-permute-start(f32[3,3,16,128]{3,2,1,0:T(8,128)S(1)} %pad_maximum_fusion.5), channel_id=1, source_target_pairs={{0,32},{32,0},{64,96},{96,64},{128,160},{160,128},{192,224},{224,1... | collective-permute-start | bytes 221192 | tf_op jit(solution)/shard_map/ppermute | solution.py:38
  49.8 0.0 collective-permute-start.14
  49.8 2.5 %body.1 = (f32[3,160,128]{2,1,0:T(8,128)S(1)}, f32[3,8,128]{2,1,0:T(8,128)S(1)}) custom-call(s32[1]{0:T(128)} %bitcast.place_ref, f32[3,160,128]{2,1,0:T(8,128)S(1)} %bitcast.471, f32[3,160,128]{2,1,0:T(8,128)S(1)} %bitcast.473, f32[160,128]{1,0:T(8,128)S(1)} %bitcast.476), custom_call_target="tpu_custom_call" | custom-call | flops 6000000 | bytes 900000 | tf_op jit(solution)/shard_map/body/pallas_call | solution.py:103
  52.4 1.2 %collective-permute-done.14 = f32[3,3,16,128]{3,2,1,0:T(8,128)S(1)} collective-permute-done((f32[3,3,16,128]{3,2,1,0:T(8,128)S(1)}, f32[3,3,16,128]{3,2,1,0:T(8,128)S(1)}, u32[]{:S(2)}, u32[]{:S(2)}) %collective-permute-start.14) | collective-permute-done | bytes 73760 | tf_op jit(solution)/shard_map/ppermute | solution.py:38
  53.6 2.9 %collective-permute-start.16 = (f32[2,3,16,128]{3,2,1,0:T(8,128)S(1)}, f32[2,3,16,128]{3,2,1,0:T(8,128)S(1)}, u32[]{:S(2)}, u32[]{:S(2)}) collective-permute-start(f32[2,3,16,128]{3,2,1,0:T(8,128)S(1)} %pad_maximum_fusion.9), channel_id=1, source_target_pairs={{0,1},{1,2},{2,3},{3,4},{4,5},{5,6},{6,7},{7,0},{8,9},{9,10},{10,1... | collective-permute-start | bytes 147464 | tf_op jit(solution)/shard_map/ppermute | solution.py:38
  56.6 0.3 collective-permute-start.17
  57.0 1.3 %collective-permute-done.16.refs_3_ = f32[2,3,16,128]{3,2,1,0:T(8,128)S(1)} collective-permute-done((f32[2,3,16,128]{3,2,1,0:T(8,128)S(1)}, f32[2,3,16,128]{3,2,1,0:T(8,128)S(1)}, u32[]{:S(2)}, u32[]{:S(2)}) %collective-permute-start.16) | collective-permute-done | bytes 49184 | tf_op jit(solution)/shard_map/ppermute | solution.py:38
  58.3 1.9 %collective-permute-done.17.refs_4_ = f32[2,3,16,128]{3,2,1,0:T(8,128)S(1)} collective-permute-done((f32[2,3,16,128]{3,2,1,0:T(8,128)S(1)}, f32[2,3,16,128]{3,2,1,0:T(8,128)S(1)}, u32[]{:S(2)}, u32[]{:S(2)}) %collective-permute-start.17) | collective-permute-done | bytes 49184 | tf_op jit(solution)/shard_map/ppermute | solution.py:38
  60.2 0.9 %edge.5 = (f32[3,16,128]{2,1,0:T(8,128)S(1)}, f32[256,128]{1,0:T(8,128)}) custom-call(f32[9,16,128]{2,1,0:T(8,128)S(1)} %load.1.refs_0_, f32[3,16,128]{2,1,0:T(8,128)S(1)} %get-tuple-element.14.refs_1_, f32[2,4,16,128]{3,2,1,0:T(8,128)S(1)} %get-tuple-element.13.refs_2_, f32[2,3,16,128]{3,2,1,0:T(8,128)S(1)} %collective-permute-done.16.refs_3_, ...), custom_call_target="tpu_custom_call" | custom-call | tf_op jit(solution)/shard_map/edge/pallas_call | solution.py:241
  61.1 8.5 %all-to-all-start = ((f32[256,1,128]{2,1,0:T(1,128)}), f32[256,1,128]{2,1,0:T(1,128)S(1)}, u32[]{:S(2)}, u32[]{:S(2)}) async-start(f32[256,1,128]{2,1,0:T(1,128)} %bitcast.97), calls=%async_computation | async-start | bytes 262144 | tf_op jit(solution)/shard_map/all_to_all | solution.py:318
  69.6 0.7 copy.12
  70.3 12.3 %all-to-all-done = f32[256,1,128]{2,1,0:T(1,128)S(1)} async-done(((f32[256,1,128]{2,1,0:T(1,128)}), f32[256,1,128]{2,1,0:T(1,128)S(1)}, u32[]{:S(2)}, u32[]{:S(2)}) %all-to-all-start) | async-done | bytes 131104 | tf_op jit(solution)/shard_map/all_to_all | solution.py:318
  82.7 0.5 slice_bitcast_fusion.18
  (46 shorter events, 0.8 us)
Async XLA Ops:
  2.4 5.1 %collective-permute-start.1 = (f32[9,16,128]{2,1,0:T(8,128)S(1)}, f32[9,16,128]{2,1,0:T(8,128)S(1)}, u32[]{:S(2)}, u32[]{:S(2)}) collective-permute-start(f32[9,16,128]{2,1,0:T(8,128)S(1)} %load.1.refs_0_), channel_id=1, source_target_pairs={{8,0},{16,8},{24,16},{0,24},{9,1},{17,9},{25,17},{1,25},{10,2},{18... | collective-permute-start | bytes 221192 | tf_op jit(solution)/shard_map/ppermute | solution.py:38
  6.0 4.4 %collective-permute-start = (f32[9,16,128]{2,1,0:T(8,128)S(1)}, f32[9,16,128]{2,1,0:T(8,128)S(1)}, u32[]{:S(2)}, u32[]{:S(2)}) collective-permute-start(f32[9,16,128]{2,1,0:T(8,128)S(1)} %load.1.refs_0_), channel_id=1, source_target_pairs={{0,8},{8,16},{16,24},{24,0},{1,9},{9,17},{17,25},{25,1},{2,10},{10... | collective-permute-start | bytes 221192 | tf_op jit(solution)/shard_map/ppermute | solution.py:38
  10.5 7.2 %collective-permute-start.3 = (f32[3,9,16,128]{3,2,1,0:T(8,128)S(1)}, f32[3,9,16,128]{3,2,1,0:T(8,128)S(1)}, u32[]{:S(2)}, u32[]{:S(2)}) collective-permute-start(f32[3,9,16,128]{3,2,1,0:T(8,128)S(1)} %pad_maximum_fusion), channel_id=1, source_target_pairs={{0,224},{32,64},{64,32},{96,128},{128,96},{160,192},{192,160},{224... | collective-permute-start | bytes 663560 | tf_op jit(solution)/shard_map/ppermute | solution.py:38
  13.8 3.9 %collective-permute-start.2 = (f32[3,9,16,128]{3,2,1,0:T(8,128)S(1)}, f32[3,9,16,128]{3,2,1,0:T(8,128)S(1)}, u32[]{:S(2)}, u32[]{:S(2)}) collective-permute-start(f32[3,9,16,128]{3,2,1,0:T(8,128)S(1)} %pad_maximum_fusion), channel_id=1, source_target_pairs={{0,32},{32,0},{64,96},{96,64},{128,160},{160,128},{192,224},{224,1... | collective-permute-start | bytes 663560 | tf_op jit(solution)/shard_map/ppermute | solution.py:38
  18.0 7.8 %collective-permute-start.4 = (f32[2,7,16,128]{3,2,1,0:T(8,128)S(1)}, f32[2,7,16,128]{3,2,1,0:T(8,128)S(1)}, u32[]{:S(2)}, u32[]{:S(2)}) collective-permute-start(f32[2,7,16,128]{3,2,1,0:T(8,128)S(1)} %pad_maximum_fusion.1), channel_id=1, source_target_pairs={{0,1},{1,2},{2,3},{3,4},{4,5},{5,6},{6,7},{7,0},{8,9},{9,10},{10,1... | collective-permute-start | bytes 344072 | tf_op jit(solution)/shard_map/ppermute | solution.py:38
  19.8 6.0 %collective-permute-start.5 = (f32[2,7,16,128]{3,2,1,0:T(8,128)S(1)}, f32[2,7,16,128]{3,2,1,0:T(8,128)S(1)}, u32[]{:S(2)}, u32[]{:S(2)}) collective-permute-start(f32[2,7,16,128]{3,2,1,0:T(8,128)S(1)} %pad_maximum_fusion.2), channel_id=1, source_target_pairs={{1,0},{2,1},{3,2},{4,3},{5,4},{6,5},{7,6},{0,7},{9,8},{10,9},{11,1... | collective-permute-start | bytes 344072 | tf_op jit(solution)/shard_map/ppermute | solution.py:38
  26.0 2.8 %collective-permute-start.7 = (f32[3,16,128]{2,1,0:T(8,128)S(1)}, f32[3,16,128]{2,1,0:T(8,128)S(1)}, u32[]{:S(2)}, u32[]{:S(2)}) collective-permute-start(f32[3,16,128]{2,1,0:T(8,128)S(1)} %get-tuple-element.12.refs_1_), channel_id=1, source_target_pairs={{8,0},{16,8},{24,16},{0,24},{9,1},{17,9},{25,17},{1,25},{10,2},{18... | collective-permute-start | bytes 73736 | tf_op jit(solution)/shard_map/ppermute | solution.py:38
  26.1 4.0 %collective-permute-start.6 = (f32[3,16,128]{2,1,0:T(8,128)S(1)}, f32[3,16,128]{2,1,0:T(8,128)S(1)}, u32[]{:S(2)}, u32[]{:S(2)}) collective-permute-start(f32[3,16,128]{2,1,0:T(8,128)S(1)} %get-tuple-element.12.refs_1_), channel_id=1, source_target_pairs={{0,8},{8,16},{16,24},{24,0},{1,9},{9,17},{17,25},{25,1},{2,10},{10... | collective-permute-start | bytes 73736 | tf_op jit(solution)/shard_map/ppermute | solution.py:38
  30.1 4.5 %collective-permute-start.9 = (f32[3,3,16,128]{3,2,1,0:T(8,128)S(1)}, f32[3,3,16,128]{3,2,1,0:T(8,128)S(1)}, u32[]{:S(2)}, u32[]{:S(2)}) collective-permute-start(f32[3,3,16,128]{3,2,1,0:T(8,128)S(1)} %pad_maximum_fusion.4), channel_id=1, source_target_pairs={{0,32},{32,0},{64,96},{96,64},{128,160},{160,128},{192,224},{224,1... | collective-permute-start | bytes 221192 | tf_op jit(solution)/shard_map/ppermute | solution.py:38
  33.6 4.1 %collective-permute-start.8 = (f32[3,3,16,128]{3,2,1,0:T(8,128)S(1)}, f32[3,3,16,128]{3,2,1,0:T(8,128)S(1)}, u32[]{:S(2)}, u32[]{:S(2)}) collective-permute-start(f32[3,3,16,128]{3,2,1,0:T(8,128)S(1)} %pad_maximum_fusion.4), channel_id=1, source_target_pairs={{0,224},{32,64},{64,32},{96,128},{128,96},{160,192},{192,160},{224... | collective-permute-start | bytes 221192 | tf_op jit(solution)/shard_map/ppermute | solution.py:38
  37.8 4.7 %collective-permute-start.10 = (f32[2,3,16,128]{3,2,1,0:T(8,128)S(1)}, f32[2,3,16,128]{3,2,1,0:T(8,128)S(1)}, u32[]{:S(2)}, u32[]{:S(2)}) collective-permute-start(f32[2,3,16,128]{3,2,1,0:T(8,128)S(1)} %pad_maximum_fusion.6), channel_id=1, source_target_pairs={{0,1},{1,2},{2,3},{3,4},{4,5},{5,6},{6,7},{7,0},{8,9},{9,10},{10,1... | collective-permute-start | bytes 147464 | tf_op jit(solution)/shard_map/ppermute | solution.py:38
  37.9 4.6 %collective-permute-start.11 = (f32[2,3,16,128]{3,2,1,0:T(8,128)S(1)}, f32[2,3,16,128]{3,2,1,0:T(8,128)S(1)}, u32[]{:S(2)}, u32[]{:S(2)}) collective-permute-start(f32[2,3,16,128]{3,2,1,0:T(8,128)S(1)} %pad_maximum_fusion.7), channel_id=1, source_target_pairs={{1,0},{2,1},{3,2},{4,3},{5,4},{6,5},{7,6},{0,7},{9,8},{10,9},{11,1... | collective-permute-start | bytes 147464 | tf_op jit(solution)/shard_map/ppermute | solution.py:38
  41.2 8.6 %copy-start.1 = (f32[1,1,1,3,20480]{4,2,3,1,0:T(1,128)S(1)}, f32[1,1,1,3,20480]{4,2,3,1,0:T(1,128)}, u32[]{:S(2)}) copy-start(f32[1,1,1,3,20480]{4,2,3,1,0:T(1,128)} %param.6) | copy-start | bytes 737284
  41.3 8.5 %copy-start = (f32[1,1,1,3,20480]{4,2,3,1,0:T(1,128)S(1)}, f32[1,1,1,3,20480]{4,2,3,1,0:T(1,128)}, u32[]{:S(2)}) copy-start(f32[1,1,1,3,20480]{4,2,3,1,0:T(1,128)} %param.5) | copy-start | bytes 737284
  42.7 7.1 %copy-start.2 = (f32[1,1,1,20480]{3,2,1,0:T(1,128)S(1)}, f32[1,1,1,20480]{3,2,1,0:T(1,128)}, u32[]{:S(2)}) copy-start(f32[1,1,1,20480]{3,2,1,0:T(1,128)} %param.7) | copy-start | bytes 245764
  42.7 2.8 %collective-permute-start.13 = (f32[3,16,128]{2,1,0:T(8,128)S(1)}, f32[3,16,128]{2,1,0:T(8,128)S(1)}, u32[]{:S(2)}, u32[]{:S(2)}) collective-permute-start(f32[3,16,128]{2,1,0:T(8,128)S(1)} %get-tuple-element.14.refs_1_), channel_id=1, source_target_pairs={{8,0},{16,8},{24,16},{0,24},{9,1},{17,9},{25,17},{1,25},{10,2},{18... | collective-permute-start | bytes 73736 | tf_op jit(solution)/shard_map/ppermute | solution.py:38
  42.8 4.0 %collective-permute-start.12 = (f32[3,16,128]{2,1,0:T(8,128)S(1)}, f32[3,16,128]{2,1,0:T(8,128)S(1)}, u32[]{:S(2)}, u32[]{:S(2)}) collective-permute-start(f32[3,16,128]{2,1,0:T(8,128)S(1)} %get-tuple-element.14.refs_1_), channel_id=1, source_target_pairs={{0,8},{8,16},{16,24},{24,0},{1,9},{9,17},{17,25},{25,1},{2,10},{10... | collective-permute-start | bytes 73736 | tf_op jit(solution)/shard_map/ppermute | solution.py:38
  46.8 5.6 %collective-permute-start.15 = (f32[3,3,16,128]{3,2,1,0:T(8,128)S(1)}, f32[3,3,16,128]{3,2,1,0:T(8,128)S(1)}, u32[]{:S(2)}, u32[]{:S(2)}) collective-permute-start(f32[3,3,16,128]{3,2,1,0:T(8,128)S(1)} %pad_maximum_fusion.5), channel_id=1, source_target_pairs={{0,32},{32,0},{64,96},{96,64},{128,160},{160,128},{192,224},{224,1... | collective-permute-start | bytes 221192 | tf_op jit(solution)/shard_map/ppermute | solution.py:38
  49.8 3.8 %collective-permute-start.14 = (f32[3,3,16,128]{3,2,1,0:T(8,128)S(1)}, f32[3,3,16,128]{3,2,1,0:T(8,128)S(1)}, u32[]{:S(2)}, u32[]{:S(2)}) collective-permute-start(f32[3,3,16,128]{3,2,1,0:T(8,128)S(1)} %pad_maximum_fusion.5), channel_id=1, source_target_pairs={{0,224},{32,64},{64,32},{96,128},{128,96},{160,192},{192,160},{224... | collective-permute-start | bytes 221192 | tf_op jit(solution)/shard_map/ppermute | solution.py:38
  53.6 4.7 %collective-permute-start.16 = (f32[2,3,16,128]{3,2,1,0:T(8,128)S(1)}, f32[2,3,16,128]{3,2,1,0:T(8,128)S(1)}, u32[]{:S(2)}, u32[]{:S(2)}) collective-permute-start(f32[2,3,16,128]{3,2,1,0:T(8,128)S(1)} %pad_maximum_fusion.9), channel_id=1, source_target_pairs={{0,1},{1,2},{2,3},{3,4},{4,5},{5,6},{6,7},{7,0},{8,9},{9,10},{10,1... | collective-permute-start | bytes 147464 | tf_op jit(solution)/shard_map/ppermute | solution.py:38
  56.6 3.6 %collective-permute-start.17 = (f32[2,3,16,128]{3,2,1,0:T(8,128)S(1)}, f32[2,3,16,128]{3,2,1,0:T(8,128)S(1)}, u32[]{:S(2)}, u32[]{:S(2)}) collective-permute-start(f32[2,3,16,128]{3,2,1,0:T(8,128)S(1)} %pad_maximum_fusion.10), channel_id=1, source_target_pairs={{1,0},{2,1},{3,2},{4,3},{5,4},{6,5},{7,6},{0,7},{9,8},{10,9},{11,1... | collective-permute-start | bytes 147464 | tf_op jit(solution)/shard_map/ppermute | solution.py:38
  61.1 21.6 %all-to-all-start = ((f32[256,1,128]{2,1,0:T(1,128)}), f32[256,1,128]{2,1,0:T(1,128)S(1)}, u32[]{:S(2)}, u32[]{:S(2)}) async-start(f32[256,1,128]{2,1,0:T(1,128)} %bitcast.97), calls=%async_computation | async-start | bytes 262144 | tf_op jit(solution)/shard_map/all_to_all | solution.py:318
